TPU v7x, 32 devices: a whole 2x2x4 slice. The times are simulated.
32 devices in a mesh: expert: 8 (over z, y), tensor: 4 (over x, core).
Axes of the slice: x: 2, y: 2, z: 4, core: 2. Of those that a mesh axis runs over, the one named last changes fastest.
Arguments:
- tokens: bfloat16 [1024, 7168], P('expert', 'tensor'), may hold values from -6 to 6
- out_grad: bfloat16 [1024, 7168], P('expert', 'tensor'), may hold values from -1.5 to 1.5
- expert_ids: int32 [1024, 2], P('expert'), may hold values from 0 to 7, all different within a row; in each aligned block of 128 rows (0 to 127, 128 to 255, ...) at most 48 rows name the same one
- gate_values: bfloat16 [1024, 2], P('expert'), may hold values from 0.099609375 to 1
- w_gate: bfloat16 [8, 7168, 1024], P('expert', None, 'tensor'), may hold values from -0.0625 to 0.0625
- w_up: bfloat16 [8, 7168, 1024], P('expert', None, 'tensor'), may hold values from -0.0625 to 0.0625
- w_down: bfloat16 [8, 1024, 7168], P('expert', 'tensor'), may hold values from -0.1875 to 0.1875
Outputs:
- d_tokens: bfloat16 [1024, 7168], P('expert', 'tensor')
- d_gates: float32 [1024, 2], P('expert')
Inputs may be any that keep to these rules, and one draw needn't show every extreme that they name: `expert_ids`: each row names 2 different experts. Among the 128 rows held at one index along `expert` (one aligned block) no expert is named by more than 48 rows, and in some such block one expert is named by exactly 48.
All inputs are finite; a program needn't handle non-finite values.
Results may differ from a plain program's by a relative error of at most 0.0049.
Values may be sent and summed in bfloat16 or wider, within the bound.
A program may use at most 128 MiB of HBM per device.

v0:
```python
import jax
import jax.numpy as jnp
from jax import lax
from jax.sharding import PartitionSpec as P


def local(tokens, out_grad, expert_ids, gate_values, w_gate, w_up, w_down):
    n_experts = lax.axis_size("expert")
    tok_rows, quarter = tokens.shape
    top_count = expert_ids.shape[1]
    most_slots = 3 * tok_rows * top_count // (2 * n_experts)
    slot_count = n_experts * most_slots
    flat_ids = expert_ids.reshape(-1)
    onehot = (flat_ids[:, None] == jnp.arange(n_experts, dtype=jnp.int32)[None, :]).astype(
        jnp.int32
    )
    before = jnp.cumsum(onehot, axis=0) - onehot
    rank = jnp.sum(before * onehot, axis=1)
    slot_of = (flat_ids * most_slots + rank).reshape(tok_rows, top_count)
    matches = slot_of[None, :, :] == jnp.arange(slot_count, dtype=jnp.int32)[:, None, None]
    chooser = jnp.any(matches, axis=2).astype(jnp.bfloat16)
    send_x = jnp.dot(chooser, tokens, preferred_element_type=jnp.float32).astype(jnp.bfloat16)
    send_dy = jnp.dot(chooser, out_grad, preferred_element_type=jnp.float32).astype(jnp.bfloat16)
    gate_wide = gate_values.astype(jnp.float32)[None, :, :]
    send_g = jnp.sum(jnp.where(matches, gate_wide, 0.0), axis=(1, 2)).astype(jnp.bfloat16)
    recv_x, recv_dy, recv_g = (
        lax.all_to_all(
            send_x.reshape(n_experts, most_slots, quarter),
            "expert",
            split_axis=0,
            concat_axis=0,
            tiled=True,
        ),
        lax.all_to_all(
            send_dy.reshape(n_experts, most_slots, quarter),
            "expert",
            split_axis=0,
            concat_axis=0,
            tiled=True,
        ),
        lax.all_to_all(
            send_g.reshape(n_experts, most_slots), "expert", split_axis=0, concat_axis=0, tiled=True
        ),
    )
    rows_x = recv_x.reshape(slot_count, quarter)
    rows_dy = recv_dy.reshape(slot_count, quarter)
    gate_mat = w_gate[0]
    up_mat = w_up[0]
    down_mat = w_down[0]
    piece_x = lax.all_gather(rows_x, "tensor", axis=1, tiled=True)
    piece_dy = lax.all_gather(rows_dy, "tensor", axis=1, tiled=True)
    pre_sum = jnp.dot(piece_x, gate_mat, preferred_element_type=jnp.float32)
    up_sum = jnp.dot(piece_x, up_mat, preferred_element_type=jnp.float32)
    grad_sum = lax.dot_general(
        piece_dy, down_mat, (((1,), (1,)), ((), ())), preferred_element_type=jnp.float32
    )
    sigma = jax.nn.sigmoid(pre_sum)
    active = pre_sum * sigma
    partial_grad = jnp.sum(active * up_sum * grad_sum, axis=1)
    weight_g = recv_g.reshape(slot_count).astype(jnp.float32)
    scaled = weight_g[:, None] * grad_sum
    grad_up = (scaled * active).astype(jnp.bfloat16)
    grad_pre = (scaled * up_sum * sigma * (1.0 + pre_sum * (1.0 - sigma))).astype(jnp.bfloat16)
    contrib = lax.dot_general(
        grad_pre, gate_mat, (((1,), (1,)), ((), ())), preferred_element_type=jnp.float32
    )
    contrib = contrib + lax.dot_general(
        grad_up, up_mat, (((1,), (1,)), ((), ())), preferred_element_type=jnp.float32
    )
    slot_grad = lax.psum(partial_grad, "tensor")
    returned, returned_grad = (
        lax.all_to_all(
            contrib.reshape(n_experts, most_slots, contrib.shape[1]),
            "expert",
            split_axis=0,
            concat_axis=0,
            tiled=True,
        ),
        lax.all_to_all(
            slot_grad.reshape(n_experts, most_slots),
            "expert",
            split_axis=0,
            concat_axis=0,
            tiled=True,
        ),
    )
    slot_rows = returned.reshape(slot_count, contrib.shape[1])
    combined = jnp.sum(jnp.take(slot_rows, slot_of, axis=0), axis=1)
    d_tokens = lax.psum_scatter(combined, "tensor", scatter_dimension=1, tiled=True).astype(
        jnp.bfloat16
    )
    d_gates = jnp.take(returned_grad.reshape(slot_count), slot_of, axis=0)
    return (d_tokens, d_gates)


def solution(mesh):
    placed = (
        P("expert", "tensor"),
        P("expert", "tensor"),
        P("expert", None),
        P("expert", None),
        P("expert", None, "tensor"),
        P("expert", None, "tensor"),
        P("expert", "tensor", None),
    )
    return jax.shard_map(
        local,
        mesh=mesh,
        in_specs=placed,
        out_specs=(P("expert", "tensor"), P("expert", None)),
        check_vma=False,
    )
```

profile of v0, /device:TPU:13, one launch (start us, length us, event | category | flops | bytes accessed | tf_op | source)
XLA Modules:
  0.0 489.7 jit_solution(14696424435222848767)
XLA Ops:
  7.2 0.0 all-gather.5.cloned.1.call-start
  7.2 0.9 copy.32
  8.1 0.1 eq.42
  8.2 0.1 eq.38
  8.4 0.6 reduce-window.6
  9.0 0.2 slice_reduce_fusion
  9.2 0.1 fusion.16
  9.3 0.1 reduce_sum.39
  9.5 0.1 copy.34
  9.5 0.7 compare_select_fusion
  10.3 0.5 convolution_convert_fusion
  10.8 36.3 %all_to_all.30 = bf16[8,48,1792]{2,1,0:T(8,128)(2,1)} all-to-all(bf16[8,48,1792]{2,1,0:T(8,128)(2,1)S(1)} %bitcast.40), channel_id=1, replica_groups=mesh['expert'=8,'tensor'=4] {'expert'}, dimensions={0} | all-to-all | bytes 2752512 | tf_op jit(solution)/shard_map/all_to_all | solution.py:27
  47.1 0.0 all-gather.5.cloned.1.call-update
  47.1 0.0 all-gather.3.cloned.1.call-start
  47.2 0.5 convolution_convert_fusion.1
  47.7 35.9 %all_to_all.31 = bf16[8,48,1792]{2,1,0:T(8,128)(2,1)} all-to-all(bf16[8,48,1792]{2,1,0:T(8,128)(2,1)S(1)} %bitcast.39), channel_id=1, replica_groups=mesh['expert'=8,'tensor'=4] {'expert'}, dimensions={0} | all-to-all | bytes 2752512 | tf_op jit(solution)/shard_map/all_to_all | solution.py:34
  83.6 0.0 all-gather.3.cloned.1.call-update
  83.6 0.1 select_reduce_fusion.1
  83.8 0.1 convert_element_type.63
  83.9 8.4 %all_to_all.32 = bf16[8,1,48]{2,1,0:T(2,128)(2,1)S(1)} all-to-all(bf16[8,1,48]{2,1,0:T(2,128)(2,1)S(1)} %convert_element_type.63), channel_id=1, replica_groups=mesh['expert'=8,'tensor'=4] {'expert'}, dimensions={0} | all-to-all | bytes 1536 | tf_op jit(solution)/shard_map/all_to_all | solution.py:41
  92.3 0.1 reshape.94
  92.4 5.9 %fusion.2 = f32[384,256]{0,1:T(8,128)S(1)} fusion(bf16[384,7168]{1,0:T(8,128)(2,1)} %all-gather.5.cloned.1.call-done, bf16[1,7168,256]{2,1,0:T(8,128)(2,1)} %param.11), kind=kOutput, calls=%fused_computation.6 | convolution fusion | flops 1409286144 | bytes 9568256 | tf_op jit(solution)/shard_map/dot_general | solution.py:52
  98.3 0.5 copy-done.5
  98.8 2.1 fusion.5
  101.0 33.3 %all-gather.3.cloned.1.call-done = bf16[384,7168]{1,0:T(8,128)(2,1)} async-done(((bf16[384,1792]{1,0:T(8,128)(2,1)}), bf16[384,7168]{1,0:T(8,128)(2,1)}) %all-gather.3.cloned.1.call-update) | async-done | bytes 5505040 | tf_op jit(solution)/shard_map/all_gather | solution.py:51
  134.2 5.8 %multiply_reduce_fusion = (f32[384]{0:T(512)S(1)}, f32[384,256]{0,1:T(8,128)S(1)}) fusion(f32[384,256]{0,1:T(8,128)S(1)} %fusion.5, f32[384,256]{0,1:T(8,128)S(1)} %fusion.2, bf16[384,7168]{1,0:T(8,128)(2,1)} %all-gather.3.cloned.1.call-done, bf16[1,256,7168]{2,1,0:T(8,128)(2,1)} %param.13), kind=kOutput, calls=%fused_computation.15 | convolution fusion | flops 1409973888 | bytes 10356224 | tf_op jit(solution)/shard_map/dot_general | solution.py:54
  140.0 0.1 all_to_all.23
  140.1 5.9 %psum.7 = f32[8,1,48]{2,1,0:T(1,128)} all-reduce(f32[8,1,48]{2,1,0:T(1,128)S(1)} %all_to_all.23), channel_id=1, replica_groups=mesh['expert'=8,'tensor'=4] {'tensor'}, use_global_device_ids=true, to_apply=%region_8.9 | all-reduce | flops 384 | bytes 3072 | tf_op jit(solution)/shard_map/psum | solution.py:70
  146.0 5.5 %all-to-all-start.4 = ((f32[8,1,48]{2,1,0:T(1,128)}), f32[8,1,48]{2,1,0:T(1,128)S(1)}, u32[]{:S(2)}, u32[]{:S(2)}) async-start(f32[8,1,48]{2,1,0:T(1,128)} %psum.7), calls=%async_computation.5 | async-start | bytes 8192 | tf_op jit(solution)/shard_map/all_to_all | solution.py:79
  151.4 3.9 fusion
  155.4 5.7 %convolution_add_fusion = f32[384,7168]{1,0:T(8,128)} fusion(f32[384,7168]{1,0:T(8,128)S(1)} %fusion, bf16[1,7168,256]{2,1,0:T(8,128)(2,1)S(1)} %copy-done.3, f32[384,256]{0,1:T(8,128)S(1)} %get-tuple-element.13, f32[384]{0:T(512)S(1)} %reshape.94, f32[384,256]{0,1:T(8,128)S(1)} %fusion.2), kind=kOutput, calls=%fused_computation.2 | convolution fusion | flops 1412726784 | bytes 26478080 | tf_op jit(solution)/shard_map/dot_general | solution.py:67
  161.1 5.4 %all-to-all-start.3 = ((f32[8,48,7168]{2,1,0:T(8,128)}), f32[8,48,7168]{2,1,0:T(8,128)}, u32[]{:S(2)}, u32[]{:S(2)}) async-start(f32[8,48,7168]{2,1,0:T(8,128)} %bitcast.36), calls=%async_computation.3 | async-start | bytes 22020096 | tf_op jit(solution)/shard_map/all_to_all | solution.py:72
  166.6 0.1 copy.37
  166.7 0.1 reshape.97
  166.8 0.5 broadcast.53
  167.4 0.7 reduce.9
  168.0 0.1 reshape.93
  168.1 1.9 gather_fusion.1
  170.1 0.1 reshape.104
  170.2 0.1 copy.38
  170.3 0.6 broadcast_select_fusion
  170.9 0.1 copy.35
  171.0 232.3 %all-to-all-done.3 = f32[8,48,7168]{2,1,0:T(8,128)} async-done(((f32[8,48,7168]{2,1,0:T(8,128)}), f32[8,48,7168]{2,1,0:T(8,128)}, u32[]{:S(2)}, u32[]{:S(2)}) %all-to-all-start.3) | async-done | bytes 11010080 | tf_op jit(solution)/shard_map/all_to_all | solution.py:72
  403.3 13.0 %gather_fusion = f32[256,7168]{1,0:T(8,128)} fusion(f32[384,7168]{1,0:T(8,128)} %bitcast.10, s32[1024]{0:T(1024)S(1)} %pad_clamp_fusion), kind=kCustom, calls=%fused_computation | custom fusion | bytes 14681088 | tf_op jit(solution)/shard_map/jit(_take)/gather | solution.py:88
  416.3 9.3 %reshape.96 = f32[128,2,7168]{2,1,0:T(2,128)} reshape(f32[256,7168]{1,0:T(8,128)} %gather_fusion) | data formatting | bytes 14680064 | tf_op jit(solution)/shard_map/jit(_take)/gather | solution.py:88
  425.5 13.4 %select_reduce_fusion = f32[128,7168]{1,0:T(8,128)} fusion(f32[128,2,7168]{2,1,0:T(2,128)} %reshape.96, pred[128,2]{1,0:T(8,128)(4,1)S(1)} %copy.35), kind=kLoop, calls=%fused_computation.3 | loop fusion | flops 2752512 | bytes 11010304 | tf_op jit(solution)/shard_map/reduce_sum | solution.py:88
  439.0 42.2 %reduce-scatter.2.cloned.1.call-done = f32[128,1792]{1,0:T(8,128)} async-done(((f32[128,7168]{1,0:T(8,128)}), f32[128,1792]{1,0:T(8,128)}) %reduce-scatter.2.cloned.1.call-update) | async-done | bytes 917520 | tf_op jit(solution)/shard_map/reduce_scatter | solution.py:89
  481.2 2.0 convert_element_type.61
  (24 shorter events, 0.2 us)
Async XLA Ops:
  7.2 3.1 copy-start
  7.2 40.0 %copy-start.4 = (bf16[128,1792]{1,0:T(8,128)(2,1)S(1)}, bf16[128,1792]{1,0:T(8,128)(2,1)}, u32[]{:S(2)}) copy-start(bf16[128,1792]{1,0:T(8,128)(2,1)} %param.8) | copy-start | bytes 1376260
  7.2 85.2 %all-gather.5.cloned.1.call-start = ((), (), s32[]{:S(2)}) async-start(), calls=%async_computation.7 | async-start | bytes 6881280 | tf_op jit(solution)/shard_map/all_gather | solution.py:50
  47.1 36.5 %copy-start.6 = (bf16[128,2]{0,1:T(2,128)(2,1)S(1)}, bf16[128,2]{0,1:T(2,128)(2,1)}, u32[]{:S(2)}) copy-start(bf16[128,2]{0,1:T(2,128)(2,1)} %param.10) | copy-start | bytes 1540
  47.1 87.1 %all-gather.3.cloned.1.call-start = ((), (), s32[]{:S(2)}) async-start(), calls=%async_computation.6 | async-start | bytes 6881280 | tf_op jit(solution)/shard_map/all_gather | solution.py:51
  92.4 5.9 %copy-start.2 = (bf16[1,7168,256]{2,1,0:T(8,128)(2,1)S(1)}, bf16[1,7168,256]{2,1,0:T(8,128)(2,1)}, u32[]{:S(2)}) copy-start(bf16[1,7168,256]{2,1,0:T(8,128)(2,1)} %param.12) | copy-start | bytes 11010052
  92.4 6.4 %copy-start.5 = (bf16[384,7168]{1,0:T(8,128)(2,1)S(1)}, bf16[384,7168]{1,0:T(8,128)(2,1)}, u32[]{:S(2)}) copy-start(bf16[384,7168]{1,0:T(8,128)(2,1)} %all-gather.5.cloned.1.call-done) | copy-start | bytes 16515076
  146.0 15.2 %all-to-all-start.4 = ((f32[8,1,48]{2,1,0:T(1,128)}), f32[8,1,48]{2,1,0:T(1,128)S(1)}, u32[]{:S(2)}, u32[]{:S(2)}) async-start(f32[8,1,48]{2,1,0:T(1,128)} %psum.7), calls=%async_computation.5 | async-start | bytes 8192 | tf_op jit(solution)/shard_map/all_to_all | solution.py:79
  151.4 4.0 copy-start.3
  161.1 242.2 %all-to-all-start.3 = ((f32[8,48,7168]{2,1,0:T(8,128)}), f32[8,48,7168]{2,1,0:T(8,128)}, u32[]{:S(2)}, u32[]{:S(2)}) async-start(f32[8,48,7168]{2,1,0:T(8,128)} %bitcast.36), calls=%async_computation.3 | async-start | bytes 22020096 | tf_op jit(solution)/shard_map/all_to_all | solution.py:72
  166.6 314.6 %reduce-scatter.2.cloned.1.call-start = ((), (), s32[]{:S(2)}) async-start(), calls=%async_computation.8 | async-start | bytes 4587520 | tf_op jit(solution)/shard_map/reduce_scatter | solution.py:89
  425.5 57.7 %copy-start.1 = (bf16[128,1792]{1,0:T(8,128)(2,1)S(1)}, bf16[128,1792]{1,0:T(8,128)(2,1)}, u32[]{:S(2)}) copy-start(bf16[128,1792]{1,0:T(8,128)(2,1)} %param.7) | copy-start | bytes 1376260
Sparse Core Ops, SparseCore 0:
  47.2 43.4 all-gather.4
  92.3 41.9 all-gather.2
  439.1 42.0 reduce-scatter.1
where the time goes:
time: 492 us; the launch traced here: 490 us
  waiting for transfers between devices  308 us (63%)
  blocking collectives  86.5 us (18%)
  local copies, waits for them, and re-layouts  27.7 us (6%)
  matrix products  24.5 us (5%)
  other arithmetic  18.3 us (4%)
  between operations  13.9 us (3%)
  starting transfers between devices  11 us (2%)
    all_to_all x1, waiting for transfers between devices, local(): lax.all_to_all(contrib.reshape(n_experts, most_slots, contrib.shape[1]),...  232 us
    reduce_scatter x1, waiting for transfers between devices, local(): lax.psum_scatter(combined, 'tensor', scatter_dimension=1, tiled=True)  42.2 us
    all_to_all x1, blocking collectives, local(): lax.all_to_all(send_x.reshape(n_experts, most_slots, quarter), 'expert',...  36.3 us
    all_to_all x1, blocking collectives, local(): lax.all_to_all(send_dy.reshape(n_experts, most_slots, quarter), 'expert',...  35.9 us
    all_gather x1, waiting for transfers between devices, local(): piece_dy = lax.all_gather(rows_dy, 'tensor', axis=1, tiled=True)  33.3 us
    gather x2, local copies, waits for them, and re-layouts, local(): combined = jnp.sum(jnp.take(slot_rows, slot_of, axis=0), axis=1)  22.2 us
    reduce_sum x1, other arithmetic, local(): combined = jnp.sum(jnp.take(slot_rows, slot_of, axis=0), axis=1)  13.4 us
  transfers between devices with their start and end apart: 5, of which 3 were waited for; matrix products, arithmetic and copies ran while one was open for 5% of the time, Pallas kernels for 0%

commit v1 on v0

--- a/solution.py
+++ b/solution.py
@@ -68,28 +68,31 @@
         grad_up, up_mat, (((1,), (1,)), ((), ())), preferred_element_type=jnp.float32
     )
     slot_grad = lax.psum(partial_grad, "tensor")
-    returned, returned_grad = (
-        lax.all_to_all(
-            contrib.reshape(n_experts, most_slots, contrib.shape[1]),
-            "expert",
-            split_axis=0,
-            concat_axis=0,
-            tiled=True,
-        ),
-        lax.all_to_all(
-            slot_grad.reshape(n_experts, most_slots),
-            "expert",
-            split_axis=0,
-            concat_axis=0,
-            tiled=True,
-        ),
+    shares = lax.psum_scatter(
+        contrib.astype(jnp.bfloat16), "tensor", scatter_dimension=1, tiled=True
     )
-    slot_rows = returned.reshape(slot_count, contrib.shape[1])
-    combined = jnp.sum(jnp.take(slot_rows, slot_of, axis=0), axis=1)
-    d_tokens = lax.psum_scatter(combined, "tensor", scatter_dimension=1, tiled=True).astype(
-        jnp.bfloat16
+    returned = lax.all_to_all(
+        shares.reshape(n_experts, most_slots, quarter),
+        "expert",
+        split_axis=0,
+        concat_axis=0,
+        tiled=True,
     )
-    d_gates = jnp.take(returned_grad.reshape(slot_count), slot_of, axis=0)
+    returned_grad = lax.all_to_all(
+        slot_grad.reshape(n_experts, most_slots),
+        "expert",
+        split_axis=0,
+        concat_axis=0,
+        tiled=True,
+    )
+    d_tokens = lax.dot_general(
+        chooser,
+        returned.reshape(slot_count, quarter),
+        (((0,), (0,)), ((), ())),
+        preferred_element_type=jnp.float32,
+    ).astype(jnp.bfloat16)
+    grad_wide = returned_grad.reshape(slot_count)[:, None, None]
+    d_gates = jnp.sum(jnp.where(matches, grad_wide, 0.0), axis=0)
     return (d_tokens, d_gates)
 
 

time: 492 us -> 276 us (0.56)
  waiting for transfers between devices: 308 us -> 101 us
  blocking collectives: 86.5 us -> 122 us
  local copies, waits for them, and re-layouts: 27.7 us -> 2.84 us
  other arithmetic: 18.3 us -> 2.86 us
  starting transfers between devices: 11 us -> 5.56 us
    all_to_all x1 -> x0, waiting for transfers between devices: 232 us -> none  [local(): lax.all_to_all(contrib.reshape(n_experts, most_slots, contrib.shape[1]),...]
    all_to_all x0 -> x1, blocking collectives: none -> 36.1 us  [local(): lax.all_to_all(shares.reshape(n_experts, most_slots, quarter), 'expert',...]
    gather x5 -> x0, local copies, waits for them, and re-layouts: 24.4 us -> none  [the longest x2 22.2 us: local(): combined = jnp.sum(jnp.take(slot_rows, slot_of, axis=0), axis=1)]
    reduce_scatter x1, waiting for transfers between devices: 42.2 us -> 55.3 us  [local(): lax.psum_scatter(contrib.astype(jnp.bfloat16), 'tensor', scatter_dimensio...]
    reduce_sum x2 -> x1, other arithmetic: 13.6 us -> 0.71 us  [local(): d_gates = jnp.sum(jnp.where(matches, grad_wide, 0.0), axis=0)]
    all_gather x1, waiting for transfers between devices: 0.01 us -> 7.11 us  [local(): piece_x = lax.all_gather(rows_x, 'tensor', axis=1, tiled=True)]
    all_to_all x1 -> x0, starting transfers between devices: 5.44 us -> none  [local(): lax.all_to_all(contrib.reshape(n_experts, most_slots, contrib.shape[1]),...]
  transfers between devices with their start and end apart: 5 -> 4, of which waited for: 3 -> 4; matrix products, arithmetic and copies ran while one was open for 5% -> 3% of each run, Pallas kernels for 0% -> 0%
where the time goes in v1:
time: 276 us; the launch traced here: 272 us
  blocking collectives  122 us (44%)
  waiting for transfers between devices  101 us (37%)
  matrix products  24.1 us (9%)
  between operations  13.9 us (5%)
  starting transfers between devices  5.56 us (2%)
  other arithmetic  2.86 us (1%)
  local copies, waits for them, and re-layouts  2.84 us (1%)
    reduce_scatter x1, waiting for transfers between devices, local(): lax.psum_scatter(contrib.astype(jnp.bfloat16), 'tensor', scatter_dimensio...  55.3 us
    all_to_all x1, blocking collectives, local(): lax.all_to_all(send_x.reshape(n_experts, most_slots, quarter), 'expert',...  36.3 us
    all_to_all x1, blocking collectives, local(): lax.all_to_all(shares.reshape(n_experts, most_slots, quarter), 'expert',...  36.1 us
    all_to_all x1, blocking collectives, local(): lax.all_to_all(send_dy.reshape(n_experts, most_slots, quarter), 'expert',...  35.9 us
    all_gather x1, waiting for transfers between devices, local(): piece_dy = lax.all_gather(rows_dy, 'tensor', axis=1, tiled=True)  35.1 us
    all_to_all x1, blocking collectives, local(): lax.all_to_all(send_g.reshape(n_experts, most_slots), 'expert', split_axi...  7.67 us
    all_gather x1, waiting for transfers between devices, local(): piece_x = lax.all_gather(rows_x, 'tensor', axis=1, tiled=True)  7.11 us
    dot_general x1, matrix products, local(): pre_sum = jnp.dot(piece_x, gate_mat, preferred_element_type=jnp.float32)  5.91 us
  transfers between devices with their start and end apart: 4, of which 4 were waited for; matrix products, arithmetic and copies ran while one was open for 3% of the time, Pallas kernels for 0%

profile of v1, /device:TPU:13, one launch (start us, length us, event | category | flops | bytes accessed | tf_op | source)
XLA Modules:
  0.0 271.7 jit_solution(810567907580985810)
XLA Ops:
  7.2 0.0 copy-start
  7.2 0.0 copy-start.3
  7.2 0.0 all-gather.5.cloned.1.call-start
  7.2 0.9 copy.28
  8.1 0.1 eq.42
  8.2 0.1 eq.38
  8.4 0.6 reduce-window.6
  9.0 0.2 slice_reduce_fusion
  9.2 0.1 fusion.16
  9.3 0.1 reduce_sum.39
  9.5 0.1 copy.30
  9.5 0.7 multiply_add_fusion
  10.3 0.0 copy-done
  10.3 0.5 convolution_convert_fusion
  10.8 36.3 %all_to_all.30 = bf16[8,48,1792]{2,1,0:T(8,128)(2,1)} all-to-all(bf16[8,48,1792]{2,1,0:T(8,128)(2,1)S(1)} %bitcast.41), channel_id=1, replica_groups=mesh['expert'=8,'tensor'=4] {'expert'}, dimensions={0} | all-to-all | bytes 2752512 | tf_op jit(solution)/shard_map/all_to_all | solution.py:27
  47.1 0.0 all-gather.5.cloned.1.call-update
  47.1 0.0 all-gather.3.cloned.1.call-start
  47.1 0.0 copy-done.3
  47.2 0.5 convolution_convert_fusion.1
  47.7 35.9 %all_to_all.31 = bf16[8,48,1792]{2,1,0:T(8,128)(2,1)} all-to-all(bf16[8,48,1792]{2,1,0:T(8,128)(2,1)S(1)} %bitcast.42), channel_id=1, replica_groups=mesh['expert'=8,'tensor'=4] {'expert'}, dimensions={0} | all-to-all | bytes 2752512 | tf_op jit(solution)/shard_map/all_to_all | solution.py:34
  83.6 0.0 all-gather.3.cloned.1.call-update
  83.6 7.1 %all-gather.5.cloned.1.call-done = bf16[384,7168]{1,0:T(8,128)(2,1)} async-done(((bf16[384,1792]{1,0:T(8,128)(2,1)}), bf16[384,7168]{1,0:T(8,128)(2,1)}) %all-gather.5.cloned.1.call-update) | async-done | bytes 5505040 | tf_op jit(solution)/shard_map/all_gather | solution.py:50
  90.7 5.9 %fusion.2 = f32[384,256]{0,1:T(8,128)S(1)} fusion(bf16[384,7168]{1,0:T(8,128)(2,1)} %all-gather.5.cloned.1.call-done, bf16[1,7168,256]{2,1,0:T(8,128)(2,1)} %param.11), kind=kOutput, calls=%fused_computation.3 | convolution fusion | flops 1409286144 | bytes 9568256 | tf_op jit(solution)/shard_map/dot_general | solution.py:52
  96.6 0.0 copy-done.1
  96.7 0.4 copy-done.4
  97.1 2.1 fusion.5
  99.2 0.0 copy-start.5
  99.2 35.1 %all-gather.3.cloned.1.call-done = bf16[384,7168]{1,0:T(8,128)(2,1)} async-done(((bf16[384,1792]{1,0:T(8,128)(2,1)}), bf16[384,7168]{1,0:T(8,128)(2,1)}) %all-gather.3.cloned.1.call-update) | async-done | bytes 5505040 | tf_op jit(solution)/shard_map/all_gather | solution.py:51
  134.2 5.8 %multiply_reduce_fusion = (f32[384]{0:T(512)S(1)}, f32[384,256]{0,1:T(8,128)S(1)}) fusion(f32[384,256]{0,1:T(8,128)S(1)} %fusion.5, f32[384,256]{0,1:T(8,128)S(1)} %fusion.2, bf16[384,7168]{1,0:T(8,128)(2,1)} %all-gather.3.cloned.1.call-done, bf16[1,256,7168]{2,1,0:T(8,128)(2,1)} %param.13), kind=kOutput, calls=%fused_computation.14 | convolution fusion | flops 1409973888 | bytes 10356224 | tf_op jit(solution)/shard_map/dot_general | solution.py:54
  140.0 0.1 all_to_all.23
  140.1 5.9 %psum.7 = f32[8,1,48]{2,1,0:T(1,128)} all-reduce(f32[8,1,48]{2,1,0:T(1,128)S(1)} %all_to_all.23), channel_id=1, replica_groups=mesh['expert'=8,'tensor'=4] {'tensor'}, use_global_device_ids=true, to_apply=%region_7.8 | all-reduce | flops 384 | bytes 3072 | tf_op jit(solution)/shard_map/psum | solution.py:70
  146.0 5.5 %all-to-all-start.4 = ((f32[8,1,48]{2,1,0:T(1,128)}), f32[8,1,48]{2,1,0:T(1,128)S(1)}, u32[]{:S(2)}, u32[]{:S(2)}) async-start(f32[8,1,48]{2,1,0:T(1,128)} %psum.7), calls=%async_computation.5 | async-start | bytes 8192 | tf_op jit(solution)/shard_map/all_to_all | solution.py:81
  151.4 0.0 copy-done.5
  151.5 3.1 %all-to-all-done.4 = f32[8,1,48]{2,1,0:T(1,128)S(1)} async-done(((f32[8,1,48]{2,1,0:T(1,128)}), f32[8,1,48]{2,1,0:T(1,128)S(1)}, u32[]{:S(2)}, u32[]{:S(2)}) %all-to-all-start.4) | async-done | bytes 1568 | tf_op jit(solution)/shard_map/all_to_all | solution.py:81
  154.6 0.5 broadcast.43
  155.1 0.7 reduce.9
  155.8 0.1 broadcast_in_dim.30
  155.9 0.7 select_reduce_fusion
  156.6 0.1 convert_element_type.67
  156.7 7.7 %all_to_all.32 = bf16[8,1,48]{2,1,0:T(2,128)(2,1)S(1)} all-to-all(bf16[8,1,48]{2,1,0:T(2,128)(2,1)S(1)} %convert_element_type.67), channel_id=1, replica_groups=mesh['expert'=8,'tensor'=4] {'expert'}, dimensions={0} | all-to-all | bytes 1536 | tf_op jit(solution)/shard_map/all_to_all | solution.py:41
  164.4 0.1 reshape.84
  164.4 4.0 %fusion = f32[384,7168]{1,0:T(8,128)S(1)} fusion(bf16[1,7168,256]{2,1,0:T(8,128)(2,1)} %param.11, f32[384,256]{0,1:T(8,128)S(1)} %fusion.2, f32[384,256]{0,1:T(8,128)S(1)} %fusion.5, f32[384,256]{0,1:T(8,128)S(1)} %get-tuple-element.5, f32[384]{0:T(512)S(1)} %reshape.84), kind=kOutput, calls=%fused_computation.1 | convolution fusion | flops 1410367488 | bytes 15861248 | tf_op jit(solution)/shard_map/dot_general | solution.py:64
  168.4 0.0 copy-done.2
  168.4 4.1 %add_convert_fusion = bf16[384,7168]{1,0:T(8,128)(2,1)} fusion(f32[384,7168]{1,0:T(8,128)S(1)} %fusion, bf16[1,7168,256]{2,1,0:T(8,128)(2,1)S(1)} %copy-done.2, f32[384,256]{0,1:T(8,128)S(1)} %get-tuple-element.5, f32[384]{0:T(512)S(1)} %reshape.84, f32[384,256]{0,1:T(8,128)S(1)} %fusion.2), kind=kOutput, calls=%fused_computation | convolution fusion | flops 1415479296 | bytes 20973056 | tf_op jit(solution)/shard_map/dot_general | solution.py:67
  172.5 0.0 reduce-scatter.2.cloned.1.call-update
  172.5 55.3 %reduce-scatter.2.cloned.1.call-done = bf16[384,1792]{1,0:T(8,128)(2,1)} async-done(((bf16[384,7168]{1,0:T(8,128)(2,1)}), bf16[384,1792]{1,0:T(8,128)(2,1)}) %reduce-scatter.2.cloned.1.call-update) | async-done | bytes 1376272 | tf_op jit(solution)/shard_map/reduce_scatter | solution.py:71
  227.8 36.1 %all_to_all.33 = bf16[8,48,1792]{2,1,0:T(8,128)(2,1)S(1)} all-to-all(bf16[8,48,1792]{2,1,0:T(8,128)(2,1)} %bitcast.43), channel_id=1, replica_groups=mesh['expert'=8,'tensor'=4] {'expert'}, dimensions={0} | all-to-all | bytes 2752512 | tf_op jit(solution)/shard_map/all_to_all | solution.py:74
  264.0 1.2 convolution_convert_fusion.2
  (10 shorter events, 0.1 us)
Async XLA Ops:
  7.2 3.1 %copy-start = (bf16[128,1792]{1,0:T(8,128)(2,1)S(1)}, bf16[128,1792]{1,0:T(8,128)(2,1)}, u32[]{:S(2)}) copy-start(bf16[128,1792]{1,0:T(8,128)(2,1)} %param.7) | copy-start | bytes 1376260
  7.2 40.0 %copy-start.3 = (bf16[128,1792]{1,0:T(8,128)(2,1)S(1)}, bf16[128,1792]{1,0:T(8,128)(2,1)}, u32[]{:S(2)}) copy-start(bf16[128,1792]{1,0:T(8,128)(2,1)} %param.8) | copy-start | bytes 1376260
  7.2 83.5 %all-gather.5.cloned.1.call-start = ((), (), s32[]{:S(2)}) async-start(), calls=%async_computation.7 | async-start | bytes 6881280 | tf_op jit(solution)/shard_map/all_gather | solution.py:50
  47.1 87.1 %all-gather.3.cloned.1.call-start = ((), (), s32[]{:S(2)}) async-start(), calls=%async_computation.6 | async-start | bytes 6881280 | tf_op jit(solution)/shard_map/all_gather | solution.py:51
  90.7 5.9 %copy-start.1 = (bf16[1,7168,256]{2,1,0:T(8,128)(2,1)S(1)}, bf16[1,7168,256]{2,1,0:T(8,128)(2,1)}, u32[]{:S(2)}) copy-start(bf16[1,7168,256]{2,1,0:T(8,128)(2,1)} %param.12) | copy-start | bytes 11010052
  90.7 6.3 %copy-start.4 = (bf16[384,7168]{1,0:T(8,128)(2,1)S(1)}, bf16[384,7168]{1,0:T(8,128)(2,1)}, u32[]{:S(2)}) copy-start(bf16[384,7168]{1,0:T(8,128)(2,1)} %all-gather.5.cloned.1.call-done) | copy-start | bytes 16515076
  99.2 52.3 %copy-start.5 = (bf16[128,2]{0,1:T(2,128)(2,1)S(1)}, bf16[128,2]{0,1:T(2,128)(2,1)}, u32[]{:S(2)}) copy-start(bf16[128,2]{0,1:T(2,128)(2,1)} %param.10) | copy-start | bytes 1540
  146.0 8.6 %all-to-all-start.4 = ((f32[8,1,48]{2,1,0:T(1,128)}), f32[8,1,48]{2,1,0:T(1,128)S(1)}, u32[]{:S(2)}, u32[]{:S(2)}) async-start(f32[8,1,48]{2,1,0:T(1,128)} %psum.7), calls=%async_computation.5 | async-start | bytes 8192 | tf_op jit(solution)/shard_map/all_to_all | solution.py:81
  151.4 76.4 %reduce-scatter.2.cloned.1.call-start = ((), (), s32[]{:S(2)}) async-start(), calls=%async_computation.8 | async-start | bytes 6881280 | tf_op jit(solution)/shard_map/reduce_scatter | solution.py:71
  164.4 4.0 %copy-start.2 = (bf16[1,7168,256]{2,1,0:T(8,128)(2,1)S(1)}, bf16[1,7168,256]{2,1,0:T(8,128)(2,1)}, u32[]{:S(2)}) copy-start(bf16[1,7168,256]{2,1,0:T(8,128)(2,1)} %param.12) | copy-start | bytes 11010052
Sparse Core Ops, SparseCore 0:
  47.2 43.4 all-gather.4
  92.3 41.9 all-gather.2
  172.7 55.1 reduce-scatter.1

commit v2 on v1

v2 whole, which is shorter than its diff:
```python
import functools

import jax
import jax.numpy as jnp
from jax import lax
from jax.experimental import pallas as pl
from jax.experimental.pallas import tpu as pltpu
from jax.sharding import PartitionSpec as P


MESH = pl.DeviceIdType.MESH
VMEM = pl.BlockSpec(memory_space=pltpu.VMEM)
VMEM_BYTES = 56 * 1024 * 1024


def positions(n):
    me = lax.axis_index("expert")
    share = lax.axis_index("tensor")
    pair, side = share // 2, share % 2
    return me, share, pair * 2 + 1 - side, (1 - pair) * 2 + side


def greet(n, me, share, near, far):
    barrier = pltpu.get_barrier_semaphore()

    @pl.loop(1, n)
    def _(step):
        pl.semaphore_signal(
            barrier, inc=1, device_id=(lax.rem(me + step, n), share), device_id_type=MESH
        )

    for peer in (near, far):
        pl.semaphore_signal(barrier, inc=1, device_id=(me, peer), device_id_type=MESH)
    pl.semaphore_wait(barrier, n + 1)


def remote(src, dst, sems, index, device):
    return pltpu.make_async_remote_copy(
        src_ref=src,
        dst_ref=dst,
        send_sem=sems[0].at[index],
        recv_sem=sems[1].at[index],
        device_id=device,
        device_id_type=MESH,
    )


def spread_kernel(n, x_ref, dy_ref, g_ref, x_out, dy_out, g_out, *sems):
    me, share, near, far = positions(n)
    quarter = x_ref.shape[2]
    by_group, to_near, to_far, passed, gates = (sems[2 * i : 2 * i + 2] for i in range(5))
    own = sems[10]
    pairs = ((x_ref, x_out), (dy_ref, dy_out))

    def cols(which):
        return pl.ds(pl.multiple_of(which * quarter, 128), quarter)

    def block(which, group, owner):
        return pairs[which][1].at[group, :, cols(owner)]

    def dispatch(which, source, target):
        return remote(
            pairs[which][0].at[target],
            block(which, source, share),
            by_group,
            which * n + source,
            (target, share),
        )

    def gate_copy(source, target):
        return remote(
            g_ref.at[target], g_out.at[source], gates, source, (target, share)
        )

    def along(which, group, sent, sems_of, peer):
        return remote(
            block(which, group, sent),
            block(which, group, sent),
            sems_of,
            which * n + group,
            (me, peer),
        )

    greet(n, me, share, near, far)
    own_copies = [
        pltpu.make_async_copy(src.at[me], block(which, me, share), own.at[which])
        for which, (src, _) in enumerate(pairs)
    ]
    own_copies.append(pltpu.make_async_copy(g_ref.at[me], g_out.at[me], own.at[2]))
    for copy in own_copies:
        copy.start()
    for which in range(2):

        @pl.loop(1, n)
        def _(step):
            target = lax.rem(me + step, n)
            dispatch(which, me, target).start()

    @pl.loop(1, n)
    def _(step):
        gate_copy(me, lax.rem(me + step, n)).start()

    for copy in own_copies:
        copy.wait()

    def share_out(which, group):
        along(which, group, share, to_far, far).start()
        along(which, group, share, to_near, near).start()

    def pass_on(which, group):
        along(which, group, far, to_far, far).wait_recv()
        along(which, group, far, passed, near).start()

    for which in range(2):
        share_out(which, me)

        @pl.loop(1, n)
        def _(step):
            group = lax.rem(me - step + n, n)
            dispatch(which, group, me).wait_recv()
            share_out(which, group)
            pass_on(which, lax.rem(me - step + 1 + n, n))

        pass_on(which, lax.rem(me + 1, n))
    for which in range(2):

        @pl.loop(0, n)
        def _(group):
            along(which, group, near, to_near, near).wait_recv()
            along(which, group, 3 - share, passed, near).wait_recv()
            along(which, group, share, to_far, far).wait_send()
            along(which, group, share, to_near, near).wait_send()
            along(which, group, far, passed, near).wait_send()

        @pl.loop(1, n)
        def _(step):
            dispatch(which, me, lax.rem(me + step, n)).wait_send()

    @pl.loop(1, n)
    def _(step):
        gate_copy(me, lax.rem(me + step, n)).wait_send()
        gate_copy(lax.rem(me - step + n, n), me).wait_recv()


def spread(send_x, send_dy, send_g):
    n, most, quarter = send_x.shape
    wide = jax.ShapeDtypeStruct((n, most, 4 * quarter), send_x.dtype)
    dma = pltpu.SemaphoreType.DMA
    return pl.pallas_call(
        functools.partial(spread_kernel, n),
        out_shape=(wide, wide, jax.ShapeDtypeStruct(send_g.shape, send_g.dtype)),
        in_specs=[VMEM] * 3,
        out_specs=[VMEM] * 3,
        scratch_shapes=[dma((2 * n,))] * 8 + [dma((n,)), dma((n,)), dma((3,))],
        compiler_params=pltpu.CompilerParams(
            collective_id=0, has_side_effects=True, vmem_limit_bytes=VMEM_BYTES
        ),
    )(send_x, send_dy, send_g)


def collect_kernel(n, c_ref, p_ref, out, grad_out, near_got, far_put, far_got, put, total,
                   part_got, part_sum, *sems):
    me, share, near, far = positions(n)
    quarter = out.shape[2]
    to_near, to_far, back, grads, parts = (sems[2 * i : 2 * i + 2] for i in range(5))
    own = sems[10]

    def cols(which):
        return pl.ds(pl.multiple_of(which * quarter, 128), quarter)

    def half(group, slot):
        wanted = near if slot == 1 else 3 - share
        return remote(
            c_ref.at[group, :, cols(wanted)],
            near_got.at[group, slot],
            to_near,
            group * 2 + slot,
            (me, near),
        )

    def across(group):
        return remote(far_put.at[group], far_got.at[group], to_far, group, (me, far))

    def home(source, target):
        return remote(put.at[target], out.at[source], back, source, (target, share))

    def grad_home(source, target):
        return remote(
            part_sum.at[target], grad_out.at[source], grads, source, (target, share)
        )

    greet(n, me, share, near, far)
    part_near = remote(p_ref, part_got.at[0], parts, 0, (me, near))
    part_near.start()

    @pl.loop(0, n)
    def _(step):
        group = lax.rem(me + 1 + step, n)
        half(group, 0).start()
        half(group, 1).start()

    part_near.wait()
    part_sum[...] = p_ref[...] + part_got[0]
    part_far = remote(part_sum, part_got.at[1], parts, 1, (me, far))
    part_far.start()
    part_far.wait()
    part_sum[...] = part_sum[...] + part_got[1]

    @pl.loop(1, n)
    def _(step):
        grad_home(me, lax.rem(me + step, n)).start()

    def pair_sum(group):
        half(group, 0).wait_recv()
        mine = c_ref[group, :, cols(far)].astype(jnp.float32)
        far_put[group] = (mine + near_got[group, 0].astype(jnp.float32)).astype(far_put.dtype)
        across(group).start()
        half(group, 1).wait_recv()
        mine = c_ref[group, :, cols(share)].astype(jnp.float32)
        total[group] = mine + near_got[group, 1].astype(jnp.float32)

    def full_sum(group):
        across(group).wait_recv()
        put[group] = (total[group] + far_got[group].astype(jnp.float32)).astype(put.dtype)

    def send_home(group):
        full_sum(group)
        home(me, group).start()

    pair_sum(lax.rem(me + 1, n))

    @pl.loop(2, n + 1)
    def _(step):
        pair_sum(lax.rem(me + step, n))
        send_home(lax.rem(me + step - 1, n))

    full_sum(me)
    own_copies = [
        pltpu.make_async_copy(put.at[me], out.at[me], own.at[0]),
        pltpu.make_async_copy(part_sum.at[me], grad_out.at[me], own.at[1]),
    ]
    for copy in own_copies:
        copy.start()
    for copy in own_copies:
        copy.wait()

    @pl.loop(0, n)
    def _(group):
        half(group, 0).wait_send()
        half(group, 1).wait_send()
        across(group).wait_send()

    @pl.loop(1, n)
    def _(step):
        target = lax.rem(me + step, n)
        source = lax.rem(me - step + n, n)
        home(me, target).wait_send()
        grad_home(me, target).wait_send()
        home(source, me).wait_recv()
        grad_home(source, me).wait_recv()


def collect(contrib, partial_grad):
    n, most, width = contrib.shape
    quarter = width // 4
    kind = contrib.dtype
    dma = pltpu.SemaphoreType.DMA
    stage = pltpu.VMEM((n, most, quarter), kind)
    return pl.pallas_call(
        functools.partial(collect_kernel, n),
        out_shape=(
            jax.ShapeDtypeStruct((n, most, quarter), kind),
            jax.ShapeDtypeStruct(partial_grad.shape, partial_grad.dtype),
        ),
        in_specs=[VMEM] * 2,
        out_specs=[VMEM] * 2,
        scratch_shapes=[
            pltpu.VMEM((n, 2, most, quarter), kind),
            stage,
            stage,
            stage,
            pltpu.VMEM((n, most, quarter), jnp.float32),
            pltpu.VMEM((2,) + partial_grad.shape, jnp.float32),
            pltpu.VMEM(partial_grad.shape, jnp.float32),
            dma((2 * n,)),
            dma((2 * n,)),
        ]
        + [dma((n,))] * 6
        + [dma((2,)), dma((2,)), dma((2,))],
        compiler_params=pltpu.CompilerParams(
            collective_id=1, has_side_effects=True, vmem_limit_bytes=VMEM_BYTES
        ),
    )(contrib, partial_grad)


def local(tokens, out_grad, expert_ids, gate_values, w_gate, w_up, w_down):
    n_experts = lax.axis_size("expert")
    tok_rows, quarter = tokens.shape
    top_count = expert_ids.shape[1]
    most_slots = 3 * tok_rows * top_count // (2 * n_experts)
    slot_count = n_experts * most_slots
    flat_ids = expert_ids.reshape(-1)
    onehot = (flat_ids[:, None] == jnp.arange(n_experts, dtype=jnp.int32)[None, :]).astype(
        jnp.int32
    )
    before = jnp.cumsum(onehot, axis=0) - onehot
    rank = jnp.sum(before * onehot, axis=1)
    slot_of = (flat_ids * most_slots + rank).reshape(tok_rows, top_count)
    matches = slot_of[None, :, :] == jnp.arange(slot_count, dtype=jnp.int32)[:, None, None]
    chooser = jnp.any(matches, axis=2).astype(jnp.bfloat16)
    send_x = jnp.dot(chooser, tokens, preferred_element_type=jnp.float32).astype(jnp.bfloat16)
    send_dy = jnp.dot(chooser, out_grad, preferred_element_type=jnp.float32).astype(jnp.bfloat16)
    gate_wide = gate_values.astype(jnp.float32)[None, :, :]
    send_g = jnp.sum(jnp.where(matches, gate_wide, 0.0), axis=(1, 2))
    piece_x, piece_dy, recv_g = spread(
        send_x.reshape(n_experts, most_slots, quarter),
        send_dy.reshape(n_experts, most_slots, quarter),
        send_g.reshape(n_experts, 1, most_slots),
    )
    piece_x = piece_x.reshape(slot_count, 4 * quarter)
    piece_dy = piece_dy.reshape(slot_count, 4 * quarter)
    gate_mat = w_gate[0]
    up_mat = w_up[0]
    down_mat = w_down[0]
    pre_sum = jnp.dot(piece_x, gate_mat, preferred_element_type=jnp.float32)
    up_sum = jnp.dot(piece_x, up_mat, preferred_element_type=jnp.float32)
    grad_sum = lax.dot_general(
        piece_dy, down_mat, (((1,), (1,)), ((), ())), preferred_element_type=jnp.float32
    )
    sigma = jax.nn.sigmoid(pre_sum)
    active = pre_sum * sigma
    partial_grad = jnp.sum(active * up_sum * grad_sum, axis=1)
    weight_g = recv_g.reshape(slot_count)
    scaled = weight_g[:, None] * grad_sum
    grad_up = (scaled * active).astype(jnp.bfloat16)
    grad_pre = (scaled * up_sum * sigma * (1.0 + pre_sum * (1.0 - sigma))).astype(jnp.bfloat16)
    contrib = lax.dot_general(
        grad_pre, gate_mat, (((1,), (1,)), ((), ())), preferred_element_type=jnp.float32
    )
    contrib = contrib + lax.dot_general(
        grad_up, up_mat, (((1,), (1,)), ((), ())), preferred_element_type=jnp.float32
    )
    returned, returned_grad = collect(
        contrib.astype(jnp.bfloat16).reshape(n_experts, most_slots, 4 * quarter),
        partial_grad.reshape(n_experts, 1, most_slots),
    )
    d_tokens = lax.dot_general(
        chooser,
        returned.reshape(slot_count, quarter),
        (((0,), (0,)), ((), ())),
        preferred_element_type=jnp.float32,
    ).astype(jnp.bfloat16)
    grad_wide = returned_grad.reshape(slot_count)[:, None, None]
    d_gates = jnp.sum(jnp.where(matches, grad_wide, 0.0), axis=0)
    return (d_tokens, d_gates)


def solution(mesh):
    placed = (
        P("expert", "tensor"),
        P("expert", "tensor"),
        P("expert", None),
        P("expert", None),
        P("expert", None, "tensor"),
        P("expert", None, "tensor"),
        P("expert", "tensor", None),
    )
    return jax.shard_map(
        local,
        mesh=mesh,
        in_specs=placed,
        out_specs=(P("expert", "tensor"), P("expert", None)),
        check_vma=False,
    )
```

time: 276 us -> 184 us (0.67); the launches traced: 272 us -> 184 us
  Pallas kernels: 0 us -> 147 us
  blocking collectives: 122 us -> 0 us
  waiting for transfers between devices: 101 us -> 0 us
  between operations: 13.9 us -> 0.82 us
  starting transfers between devices: 5.56 us -> 0 us
  matrix products: 24.1 us -> 27.7 us
    pallas_call x0 -> x2, Pallas kernels: none -> 147 us  [the longest x1 96.7 us: spread(): pl.pallas_call(functools.partial(spread_kernel, n), out_shape=(wide, wide...]
    all_to_all x4 -> x0, blocking collectives: 116 us -> none  [the longest x1 36.3 us: local(): lax.all_to_all(send_x.reshape(n_experts, most_slots, quarter), 'expert',...]
    reduce_scatter x1 -> x0, waiting for transfers between devices: 55.3 us -> none  [local(): lax.psum_scatter(contrib.astype(jnp.bfloat16), 'tensor', scatter_dimensio...]
    all_gather x2 -> x0, waiting for transfers between devices: 42.2 us -> none  [the longest x1 35.1 us: local(): piece_dy = lax.all_gather(rows_dy, 'tensor', axis=1, tiled=True)]
    psum x1 -> x0, blocking collectives: 5.86 us -> none  [local(): slot_grad = lax.psum(partial_grad, 'tensor')]
    all_to_all x1 -> x0, starting transfers between devices: 5.48 us -> none  [local(): lax.all_to_all(slot_grad.reshape(n_experts, most_slots), 'expert', split_...]
    dot_general x1, matrix products: 5.76 us -> 2.09 us  [local(): lax.dot_general(piece_dy, down_mat, (((1,), (1,)), ((), ())), preferred_e...]
    all_to_all x1 -> x0, waiting for transfers between devices: 3.15 us -> none  [local(): lax.all_to_all(slot_grad.reshape(n_experts, most_slots), 'expert', split_...]
  transfers between devices with their start and end apart: 4 -> 0, of which waited for: 4 -> 0; matrix products, arithmetic and copies ran while one was open for 3% -> 0% of each run, Pallas kernels for 0% -> 0%
where the time goes in v2:
time: 184 us
  Pallas kernels  147 us (80%)
  matrix products  27.7 us (15%)
  other arithmetic  4.33 us (2%)
  local copies, waits for them, and re-layouts  3.62 us (2%)
    pallas_call x1, Pallas kernels, spread(): pl.pallas_call(functools.partial(spread_kernel, n), out_shape=(wide, wide...  96.7 us
    pallas_call x1, Pallas kernels, collect(): pl.pallas_call(functools.partial(collect_kernel, n), out_shape=(jax.Shape...  50.6 us
    dot_general x1, matrix products, local(): pre_sum = jnp.dot(piece_x, gate_mat, preferred_element_type=jnp.float32)  5.91 us
    dot_general x1, matrix products, local(): up_sum = jnp.dot(piece_x, up_mat, preferred_element_type=jnp.float32)  4.85 us
    dot_general x1, matrix products, local(): lax.dot_general(grad_up, up_mat, (((1,), (1,)), ((), ())), preferred_elem...  4.09 us
    dot_general x1, matrix products, local(): lax.dot_general(grad_pre, gate_mat, (((1,), (1,)), ((), ())), preferred_e...  3.97 us

profile of v2, /device:TPU:13, one launch (start us, length us, event | category | flops | bytes accessed | tf_op | source)
XLA Modules:
  0.0 183.8 jit_solution(6184635635587160416)
XLA Ops:
  0.6 0.0 copy-start
  0.6 0.0 copy-start.5
  0.7 0.8 copy.21
  1.5 0.1 eq.42
  1.6 0.6 reduce-window.6
  2.2 0.2 slice_reduce_fusion
  2.5 0.1 eq.38
  2.6 0.1 fusion.16
  2.7 0.1 reduce_sum.39
  2.9 0.1 copy.23
  2.9 0.7 multiply_add_fusion
  3.7 0.0 copy-done
  3.7 1.6 convolution_convert_fusion.1
  5.3 2.7 %convolution_convert_fusion = bf16[384,1792]{1,0:T(8,128)(2,1)} fusion(pred[384,128]{1,0:T(8,128)(4,1)S(1)} %fusion.10, bf16[128,1792]{1,0:T(8,128)(2,1)} %param.8), kind=kOutput, calls=%fused_computation.10 | convolution fusion | flops 176848896 | bytes 1884160 | tf_op jit(solution)/shard_map/dot_general | solution.py:312
  8.0 0.0 copy-done.5
  8.0 0.1 select_reduce_fusion.1
  8.1 0.7 reshape.58.g_ref
  8.8 96.7 %shard_map.86 = (bf16[8,48,7168]{2,1,0:T(8,128)(2,1)}, bf16[8,48,7168]{2,1,0:T(8,128)(2,1)}, f32[8,1,48]{2,1,0:T(1,128)}) custom-call(bf16[8,48,1792]{2,1,0:T(8,128)(2,1)} %bitcast.39, bf16[8,48,1792]{2,1,0:T(8,128)(2,1)} %bitcast.40, f32[8,1,48]{2,1,0:T(1,128)} %reshape.58.g_ref), custom_call_target="tpu_custom_call" | custom-call | tf_op jit(solution)/shard_map/pallas_call | solution.py:149
  105.5 0.0 copy-start.1
  105.5 0.0 slice-start
  105.5 5.9 %fusion.2 = f32[384,256]{0,1:T(8,128)S(1)} fusion(bf16[384,7168]{1,0:T(8,128)(2,1)} %bitcast.45, bf16[1,7168,256]{2,1,0:T(8,128)(2,1)} %param.11), kind=kOutput, calls=%fused_computation.3 | convolution fusion | flops 1409286144 | bytes 9568256 | tf_op jit(solution)/shard_map/dot_general | solution.py:325
  111.4 0.0 copy-done.1
  111.4 0.0 slice-start.1
  111.4 0.0 copy-start.4
  111.4 4.9 %fusion.5 = f32[384,256]{0,1:T(8,128)S(1)} fusion(bf16[384,7168]{1,0:T(8,128)(2,1)} %bitcast.46, bf16[1,7168,256]{2,1,0:T(8,128)(2,1)S(1)} %copy-done.1), kind=kOutput, calls=%fused_computation.6 | convolution fusion | flops 1409286144 | bytes 9568256 | tf_op jit(solution)/shard_map/dot_general | solution.py:326
  116.3 0.0 slice-done
  116.3 0.0 slice-done.1
  116.3 0.0 copy-done.4
  116.3 0.0 copy-start.3
  116.3 2.1 %multiply_reduce_fusion = (f32[384]{0:T(512)S(1)}, f32[384,256]{0,1:T(8,128)S(1)}) fusion(f32[384,256]{0,1:T(8,128)S(1)} %fusion.5, f32[384,256]{0,1:T(8,128)S(1)} %fusion.2, bf16[384,7168]{1,0:T(8,128)(2,1)S(1)} %bitcast.44, bf16[1,256,7168]{2,1,0:T(8,128)(2,1)S(1)} %copy-done.4), kind=kOutput, calls=%fused_computation.14 | convolution fusion | flops 1409973888 | bytes 10356224 | tf_op jit(solution)/shard_map/dot_general | solution.py:327
  118.4 0.5 broadcast.43
  119.0 0.0 copy-done.3
  119.0 0.7 reduce.8
  119.6 0.1 mul.48
  119.7 0.0 copy-start.2
  119.7 4.0 %fusion = f32[384,7168]{1,0:T(8,128)S(1)} fusion(bf16[1,7168,256]{2,1,0:T(8,128)(2,1)} %param.11, f32[384,256]{0,1:T(8,128)S(1)} %fusion.2, f32[384,256]{0,1:T(8,128)S(1)} %fusion.5, f32[384,256]{0,1:T(8,128)S(1)} %get-tuple-element.13, f32[384]{0:T(512)S(1)} %mul.48), kind=kOutput, calls=%fused_computation.1 | convolution fusion | flops 1410367488 | bytes 15861248 | tf_op jit(solution)/shard_map/dot_general | solution.py:337
  123.7 0.0 copy-done.2
  123.7 4.1 %add_convert_fusion = bf16[384,7168]{1,0:T(8,128)(2,1)} fusion(f32[384,7168]{1,0:T(8,128)S(1)} %fusion, bf16[1,7168,256]{2,1,0:T(8,128)(2,1)S(1)} %copy-done.2, f32[384,256]{0,1:T(8,128)S(1)} %get-tuple-element.13, f32[384]{0:T(512)S(1)} %mul.48, f32[384,256]{0,1:T(8,128)S(1)} %fusion.2), kind=kOutput, calls=%fused_computation | convolution fusion | flops 1415479296 | bytes 20973056 | tf_op jit(solution)/shard_map/dot_general | solution.py:340
  127.8 0.7 reshape.62.p_ref
  128.5 50.6 %shard_map.87 = (bf16[8,48,1792]{2,1,0:T(8,128)(2,1)}, f32[8,1,48]{2,1,0:T(1,128)}) custom-call(bf16[8,48,7168]{2,1,0:T(8,128)(2,1)} %bitcast.38, f32[8,1,48]{2,1,0:T(1,128)} %reshape.62.p_ref), custom_call_target="tpu_custom_call" | custom-call | tf_op jit(solution)/shard_map/pallas_call | solution.py:269
  179.1 2.6 %convolution_convert_fusion.2 = bf16[128,1792]{1,0:T(8,128)(2,1)} fusion(pred[384,128]{1,0:T(8,128)(4,1)S(1)} %fusion.10, bf16[384,1792]{1,0:T(8,128)(2,1)} %bitcast.41), kind=kOutput, calls=%fused_computation.12 | convolution fusion | flops 176390144 | bytes 1884160 | tf_op jit(solution)/shard_map/dot_general | solution.py:347
  181.7 1.3 reduce.9
  183.0 0.1 broadcast_in_dim.29
  183.1 0.7 select_reduce_fusion
  (6 shorter events, 0.1 us)
Async XLA Ops:
  0.6 3.1 %copy-start = (bf16[128,1792]{1,0:T(8,128)(2,1)S(1)}, bf16[128,1792]{1,0:T(8,128)(2,1)}, u32[]{:S(2)}) copy-start(bf16[128,1792]{1,0:T(8,128)(2,1)} %param.7) | copy-start | bytes 1376260
  0.6 7.3 %copy-start.5 = (bf16[128,2]{0,1:T(2,128)(2,1)S(1)}, bf16[128,2]{0,1:T(2,128)(2,1)}, u32[]{:S(2)}) copy-start(bf16[128,2]{0,1:T(2,128)(2,1)} %param.10) | copy-start | bytes 1540
  105.5 5.9 %copy-start.1 = (bf16[1,7168,256]{2,1,0:T(8,128)(2,1)S(1)}, bf16[1,7168,256]{2,1,0:T(8,128)(2,1)}, u32[]{:S(2)}) copy-start(bf16[1,7168,256]{2,1,0:T(8,128)(2,1)} %param.12) | copy-start | bytes 11010052
  105.5 10.8 %slice-start = ((s8[5505024]{0:T(1024)(128)(4,1)}), s8[4194304]{0:T(1024)(128)(4,1)S(1)}, s32[]{:S(2)}) async-start(s8[5505024]{0:T(1024)(128)(4,1)} %bitcast.42), calls=%async_computation | async-start | bytes 8388608
  111.4 4.9 %slice-start.1 = ((s8[5505024]{0:T(1024)(128)(4,1)}), s8[1310720]{0:T(1024)(128)(4,1)S(1)}, s32[]{:S(2)}) async-start(s8[5505024]{0:T(1024)(128)(4,1)} %bitcast.42), calls=%async_computation.1 | async-start | bytes 2621440
  111.4 4.9 %copy-start.4 = (bf16[1,256,7168]{2,1,0:T(8,128)(2,1)S(1)}, bf16[1,256,7168]{2,1,0:T(8,128)(2,1)}, u32[]{:S(2)}) copy-start(bf16[1,256,7168]{2,1,0:T(8,128)(2,1)} %param.13) | copy-start | bytes 11010052
  116.3 2.6 %copy-start.3 = (f32[8,1,48]{2,1,0:T(1,128)S(1)}, f32[8,1,48]{2,1,0:T(1,128)}, u32[]{:S(2)}) copy-start(f32[8,1,48]{2,1,0:T(1,128)} %get-tuple-element.7) | copy-start | bytes 4612
  119.7 4.0 %copy-start.2 = (bf16[1,7168,256]{2,1,0:T(8,128)(2,1)S(1)}, bf16[1,7168,256]{2,1,0:T(8,128)(2,1)}, u32[]{:S(2)}) copy-start(bf16[1,7168,256]{2,1,0:T(8,128)(2,1)} %param.12) | copy-start | bytes 11010052

commit v3 on v2

--- a/solution.py
+++ b/solution.py
@@ -293,6 +293,372 @@
     )(contrib, partial_grad)
 
 
+def fused_kernel(n, x_ref, dy_ref, g_ref, gate_hbm, up_hbm, down_hbm, out, grad_out,
+                 x_out, dy_out, g_out, gate_w, up_w, down_w, pre, up, dz, dp, du,
+                 near_put, mine, near_got, far_put, far_got, put, part, part_got, part_sum,
+                 load, *all_sems):
+    sems, late = all_sems[:11], all_sems[11:]
+    me, share, near, far = positions(n)
+    quarter = x_ref.shape[2]
+    by_group, to_near, to_far, passed, gates = (sems[2 * i : 2 * i + 2] for i in range(5))
+    own = sems[10]
+    pairs = ((x_ref, x_out), (dy_ref, dy_out))
+
+    def cols(which):
+        return pl.ds(pl.multiple_of(which * quarter, 128), quarter)
+
+    def block(which, group, owner):
+        return pairs[which][1].at[group, :, cols(owner)]
+
+    def dispatch(which, source, target):
+        return remote(
+            pairs[which][0].at[target],
+            block(which, source, share),
+            by_group,
+            which * n + source,
+            (target, share),
+        )
+
+    def gate_copy(source, target):
+        return remote(
+            g_ref.at[target], g_out.at[source], gates, source, (target, share)
+        )
+
+    def along(which, group, sent, sems_of, peer):
+        return remote(
+            block(which, group, sent),
+            block(which, group, sent),
+            sems_of,
+            which * n + group,
+            (me, peer),
+        )
+
+    to_pair, across_sems, back, grads, parts = (late[2 * i : 2 * i + 2] for i in range(5))
+    most = x_ref.shape[1]
+    rows = n * most
+    depth = quarter // 2
+    narrow = quarter // 7
+    loads = [
+        pltpu.make_async_copy(src, dst, load.at[i])
+        for i, (src, dst) in enumerate(
+            ((gate_hbm, gate_w), (up_hbm, up_w), (down_hbm, down_w))
+        )
+    ]
+
+    def half(group, slot):
+        return remote(
+            near_put.at[slot, group],
+            near_got.at[slot, group],
+            to_pair,
+            slot * n + group,
+            (me, near),
+        )
+
+    def across(group):
+        return remote(far_put.at[group], far_got.at[group], across_sems, group, (me, far))
+
+    def home(source, target):
+        return remote(put.at[target], out.at[source], back, source, (target, share))
+
+    def grad_home(source, target):
+        return remote(
+            part_sum.at[target], grad_out.at[source], grads, source, (target, share)
+        )
+
+    def nt(left, right):
+        return lax.dot_general(
+            left, right, (((1,), (1,)), ((), ())), preferred_element_type=jnp.float32
+        )
+
+    def project(step):
+        at = pl.ds(pl.multiple_of(step * depth, 128), depth)
+        piece = x_out[:, :, at].reshape(rows, depth)
+        pre[...] += jnp.dot(piece, gate_w[at, :], preferred_element_type=jnp.float32)
+        up[...] += jnp.dot(piece, up_w[at, :], preferred_element_type=jnp.float32)
+
+    greet(n, me, share, near, far)
+    own_copies = [
+        pltpu.make_async_copy(src.at[me], block(which, me, share), own.at[which])
+        for which, (src, _) in enumerate(pairs)
+    ]
+    own_copies.append(pltpu.make_async_copy(g_ref.at[me], g_out.at[me], own.at[2]))
+    for copy in own_copies:
+        copy.start()
+    for which in range(2):
+
+        @pl.loop(1, n)
+        def _(step):
+            target = lax.rem(me + step, n)
+            dispatch(which, me, target).start()
+
+    @pl.loop(1, n)
+    def _(step):
+        gate_copy(me, lax.rem(me + step, n)).start()
+
+    for copy in loads:
+        copy.start()
+    pre[...] = jnp.zeros_like(pre)
+    up[...] = jnp.zeros_like(up)
+    dz[...] = jnp.zeros_like(dz)
+    for copy in own_copies:
+        copy.wait()
+
+    def share_out(which, group):
+        along(which, group, share, to_far, far).start()
+        along(which, group, share, to_near, near).start()
+
+    def pass_on(which, group):
+        along(which, group, far, to_far, far).wait_recv()
+        along(which, group, far, passed, near).start()
+
+    def settle(which):
+        @pl.loop(0, n)
+        def _(group):
+            along(which, group, near, to_near, near).wait_recv()
+            along(which, group, 3 - share, passed, near).wait_recv()
+
+    share_out(0, me)
+
+    @pl.loop(1, n)
+    def _(step):
+        group = lax.rem(me - step + n, n)
+        dispatch(0, group, me).wait_recv()
+        share_out(0, group)
+        pass_on(0, lax.rem(me - step + 1 + n, n))
+
+    share_out(1, me)
+    pass_on(0, lax.rem(me + 1, n))
+    settle(0)
+    loads[0].wait()
+    loads[1].wait()
+
+    @pl.loop(1, n)
+    def _(step):
+        project(step - 1)
+        group = lax.rem(me - step + n, n)
+        dispatch(1, group, me).wait_recv()
+        share_out(1, group)
+        pass_on(1, lax.rem(me - step + 1 + n, n))
+
+    @pl.loop(n - 1, 8)
+    def _(step):
+        project(step)
+
+    pass_on(1, lax.rem(me + 1, n))
+
+    @pl.loop(1, n)
+    def _(step):
+        gate_copy(lax.rem(me - step + n, n), me).wait_recv()
+
+    loads[2].wait()
+    settle(1)
+
+    @pl.loop(0, 8)
+    def _(step):
+        at = pl.ds(pl.multiple_of(step * depth, 128), depth)
+        dz[...] += nt(dy_out[:, :, at].reshape(rows, depth), down_w[:, at])
+
+    @pl.loop(0, n)
+    def _(group):
+        at = pl.ds(pl.multiple_of(group * most, 16), most)
+        pre_b, up_b, dz_b = pre[at, :], up[at, :], dz[at, :]
+        sigma = jax.nn.sigmoid(pre_b)
+        active = pre_b * sigma
+        row = jnp.sum(active * up_b * dz_b, axis=1, keepdims=True)
+        part[group] = jnp.broadcast_to(row, (most, 128))
+        scaled = g_out[group][:, :1].astype(jnp.float32) * dz_b
+        du[at, :] = (scaled * active).astype(du.dtype)
+        dp[at, :] = (scaled * up_b * sigma * (1.0 + pre_b * (1.0 - sigma))).astype(dp.dtype)
+
+    part_near = remote(part, part_got.at[0], parts, 0, (me, near))
+    part_near.start()
+
+    def expand(which, store):
+        @pl.loop(0, 7)
+        def _(step):
+            at = pl.ds(pl.multiple_of(which * quarter + step * narrow, 128), narrow)
+            value = nt(dp[...], gate_w[at, :]) + nt(du[...], up_w[at, :])
+            store(
+                pl.ds(pl.multiple_of(step * narrow, 128), narrow),
+                value.reshape(n, most, narrow),
+            )
+
+    for slot, wanted in ((0, 3 - share), (1, near)):
+
+        def keep(at, value):
+            near_put[slot, :, :, at] = value.astype(near_put.dtype)
+
+        expand(wanted, keep)
+
+        @pl.loop(0, n)
+        def _(step):
+            half(lax.rem(me + 1 + step, n), slot).start()
+
+    for slot, wanted in ((0, far), (1, share)):
+
+        def keep_wide(at, value):
+            mine[slot, :, :, at] = value
+
+        expand(wanted, keep_wide)
+        if slot == 0:
+            part_near.wait()
+            part_sum[...] = part[...] + part_got[0]
+            part_far = remote(part_sum, part_got.at[1], parts, 1, (me, far))
+            part_far.start()
+
+            @pl.loop(0, n)
+            def _(step):
+                group = lax.rem(me + 1 + step, n)
+                half(group, 0).wait_recv()
+                far_put[group] = (
+                    mine[0, group] + near_got[0, group].astype(jnp.float32)
+                ).astype(far_put.dtype)
+                across(group).start()
+
+    part_far.wait()
+    part_sum[...] = part_sum[...] + part_got[1]
+
+    @pl.loop(1, n)
+    def _(step):
+        grad_home(me, lax.rem(me + step, n)).start()
+
+    def full_sum(group):
+        half(group, 1).wait_recv()
+        across(group).wait_recv()
+        pair = mine[1, group] + near_got[1, group].astype(jnp.float32)
+        put[group] = (pair + far_got[group].astype(jnp.float32)).astype(put.dtype)
+
+    @pl.loop(1, n)
+    def _(step):
+        group = lax.rem(me + step, n)
+        full_sum(group)
+        home(me, group).start()
+
+    full_sum(me)
+    last_copies = [
+        pltpu.make_async_copy(put.at[me], out.at[me], own.at[0]),
+        pltpu.make_async_copy(part_sum.at[me], grad_out.at[me], own.at[1]),
+    ]
+    for copy in last_copies:
+        copy.start()
+    for copy in last_copies:
+        copy.wait()
+    for which in range(2):
+
+        @pl.loop(0, n)
+        def _(group):
+            along(which, group, share, to_far, far).wait_send()
+            along(which, group, share, to_near, near).wait_send()
+            along(which, group, far, passed, near).wait_send()
+            half(group, which).wait_send()
+
+        @pl.loop(1, n)
+        def _(step):
+            dispatch(which, me, lax.rem(me + step, n)).wait_send()
+
+    @pl.loop(0, n)
+    def _(group):
+        across(group).wait_send()
+
+    @pl.loop(1, n)
+    def _(step):
+        target = lax.rem(me + step, n)
+        source = lax.rem(me - step + n, n)
+        gate_copy(me, target).wait_send()
+        home(me, target).wait_send()
+        grad_home(me, target).wait_send()
+        home(source, me).wait_recv()
+        grad_home(source, me).wait_recv()
+
+
+def fused(send_x, send_dy, send_g, gate_mat, up_mat, down_mat):
+    n, most, quarter = send_x.shape
+    kind = send_x.dtype
+    hidden = gate_mat.shape[1]
+    rows = n * most
+    dma = pltpu.SemaphoreType.DMA
+    wide = pltpu.VMEM((n, most, 4 * quarter), kind)
+    square = pltpu.VMEM((rows, hidden), jnp.float32)
+    stage = pltpu.VMEM((n, most, quarter), kind)
+    flat = (n, most, 128)
+    anywhere = pl.BlockSpec(memory_space=pl.ANY)
+    return pl.pallas_call(
+        functools.partial(fused_kernel, n),
+        out_shape=(
+            jax.ShapeDtypeStruct((n, most, quarter), kind),
+            jax.ShapeDtypeStruct(flat, jnp.float32),
+        ),
+        in_specs=[VMEM] * 3 + [anywhere] * 3,
+        out_specs=[VMEM] * 2,
+        scratch_shapes=[
+            wide,
+            wide,
+            pltpu.VMEM(flat, kind),
+            pltpu.VMEM(gate_mat.shape, kind),
+            pltpu.VMEM(up_mat.shape, kind),
+            pltpu.VMEM(down_mat.shape, kind),
+            square,
+            square,
+            square,
+            pltpu.VMEM((rows, hidden), kind),
+            pltpu.VMEM((rows, hidden), kind),
+            pltpu.VMEM((2, n, most, quarter), kind),
+            pltpu.VMEM((2, n, most, quarter), jnp.float32),
+            pltpu.VMEM((2, n, most, quarter), kind),
+            stage,
+            stage,
+            stage,
+            pltpu.VMEM(flat, jnp.float32),
+            pltpu.VMEM((2,) + flat, jnp.float32),
+            pltpu.VMEM(flat, jnp.float32),
+            dma((3,)),
+        ]
+        + [dma((2 * n,))] * 8
+        + [dma((n,)), dma((n,)), dma((3,))]
+        + [dma((2 * n,))] * 2
+        + [dma((n,))] * 6
+        + [dma((2,))] * 2,
+        compiler_params=pltpu.CompilerParams(
+            collective_id=2, has_side_effects=True, vmem_limit_bytes=VMEM_BYTES
+        ),
+    )(send_x, send_dy, send_g, gate_mat, up_mat, down_mat)
+
+
+def in_steps(send_x, send_dy, send_g, gate_mat, up_mat, down_mat):
+    n_experts, most_slots, quarter = send_x.shape
+    slot_count = n_experts * most_slots
+    piece_x, piece_dy, recv_g = spread(
+        send_x,
+        send_dy,
+        send_g.reshape(n_experts, 1, most_slots),
+    )
+    piece_x = piece_x.reshape(slot_count, 4 * quarter)
+    piece_dy = piece_dy.reshape(slot_count, 4 * quarter)
+    pre_sum = jnp.dot(piece_x, gate_mat, preferred_element_type=jnp.float32)
+    up_sum = jnp.dot(piece_x, up_mat, preferred_element_type=jnp.float32)
+    grad_sum = lax.dot_general(
+        piece_dy, down_mat, (((1,), (1,)), ((), ())), preferred_element_type=jnp.float32
+    )
+    sigma = jax.nn.sigmoid(pre_sum)
+    active = pre_sum * sigma
+    partial_grad = jnp.sum(active * up_sum * grad_sum, axis=1)
+    weight_g = recv_g.reshape(slot_count)
+    scaled = weight_g[:, None] * grad_sum
+    grad_up = (scaled * active).astype(jnp.bfloat16)
+    grad_pre = (scaled * up_sum * sigma * (1.0 + pre_sum * (1.0 - sigma))).astype(jnp.bfloat16)
+    contrib = lax.dot_general(
+        grad_pre, gate_mat, (((1,), (1,)), ((), ())), preferred_element_type=jnp.float32
+    )
+    contrib = contrib + lax.dot_general(
+        grad_up, up_mat, (((1,), (1,)), ((), ())), preferred_element_type=jnp.float32
+    )
+    returned, returned_grad = collect(
+        contrib.astype(jnp.bfloat16).reshape(n_experts, most_slots, 4 * quarter),
+        partial_grad.reshape(n_experts, 1, most_slots),
+    )
+    return returned, returned_grad
+
+
 def local(tokens, out_grad, expert_ids, gate_values, w_gate, w_up, w_down):
     n_experts = lax.axis_size("expert")
     tok_rows, quarter = tokens.shape
@@ -312,38 +678,18 @@
     send_dy = jnp.dot(chooser, out_grad, preferred_element_type=jnp.float32).astype(jnp.bfloat16)
     gate_wide = gate_values.astype(jnp.float32)[None, :, :]
     send_g = jnp.sum(jnp.where(matches, gate_wide, 0.0), axis=(1, 2))
-    piece_x, piece_dy, recv_g = spread(
-        send_x.reshape(n_experts, most_slots, quarter),
-        send_dy.reshape(n_experts, most_slots, quarter),
-        send_g.reshape(n_experts, 1, most_slots),
-    )
-    piece_x = piece_x.reshape(slot_count, 4 * quarter)
-    piece_dy = piece_dy.reshape(slot_count, 4 * quarter)
-    gate_mat = w_gate[0]
-    up_mat = w_up[0]
-    down_mat = w_down[0]
-    pre_sum = jnp.dot(piece_x, gate_mat, preferred_element_type=jnp.float32)
-    up_sum = jnp.dot(piece_x, up_mat, preferred_element_type=jnp.float32)
-    grad_sum = lax.dot_general(
-        piece_dy, down_mat, (((1,), (1,)), ((), ())), preferred_element_type=jnp.float32
-    )
-    sigma = jax.nn.sigmoid(pre_sum)
-    active = pre_sum * sigma
-    partial_grad = jnp.sum(active * up_sum * grad_sum, axis=1)
-    weight_g = recv_g.reshape(slot_count)
-    scaled = weight_g[:, None] * grad_sum
-    grad_up = (scaled * active).astype(jnp.bfloat16)
-    grad_pre = (scaled * up_sum * sigma * (1.0 + pre_sum * (1.0 - sigma))).astype(jnp.bfloat16)
-    contrib = lax.dot_general(
-        grad_pre, gate_mat, (((1,), (1,)), ((), ())), preferred_element_type=jnp.float32
-    )
-    contrib = contrib + lax.dot_general(
-        grad_up, up_mat, (((1,), (1,)), ((), ())), preferred_element_type=jnp.float32
-    )
-    returned, returned_grad = collect(
-        contrib.astype(jnp.bfloat16).reshape(n_experts, most_slots, 4 * quarter),
-        partial_grad.reshape(n_experts, 1, most_slots),
-    )
+    send_x = send_x.reshape(n_experts, most_slots, quarter)
+    send_dy = send_dy.reshape(n_experts, most_slots, quarter)
+    weights = (w_gate[0], w_up[0], w_down[0])
+    if most_slots % 16 == 0 and n_experts <= 9 and quarter % 1792 == 0:
+        wide_g = jnp.broadcast_to(
+            send_g.astype(jnp.bfloat16).reshape(n_experts, most_slots, 1),
+            (n_experts, most_slots, 128),
+        )
+        returned, returned_grad = fused(send_x, send_dy, wide_g, *weights)
+        returned_grad = returned_grad[:, :, 0]
+    else:
+        returned, returned_grad = in_steps(send_x, send_dy, send_g, *weights)
     d_tokens = lax.dot_general(
         chooser,
         returned.reshape(slot_count, quarter),

time: 184 us -> 158 us (0.86)
  matrix products: 27.7 us -> 5.81 us
    dot_general x5 -> x0, matrix products: 20.9 us -> none  [the longest x1 5.91 us: local(): pre_sum = jnp.dot(piece_x, gate_mat, preferred_element_type=jnp.float32)]
    pallas_call x2 -> x0, other arithmetic: 2 us -> none  [the longest x1 1.34 us: collect(): pl.pallas_call(functools.partial(collect_kernel, n), out_shape=(jax.Shape...]
    pallas_call x2 -> x1, Pallas kernels: 147 us -> 146 us  [fused(): pl.pallas_call(functools.partial(fused_kernel, n), out_shape=(jax.ShapeDt...]
where the time goes in v3:
time: 158 us
  Pallas kernels  146 us (92%)
  matrix products  5.81 us (4%)
  other arithmetic  3.07 us (2%)
  local copies, waits for them, and re-layouts  2.54 us (2%)
    pallas_call x1, Pallas kernels, fused(): pl.pallas_call(functools.partial(fused_kernel, n), out_shape=(jax.ShapeDt...  146 us

profile of v3, /device:TPU:13, one launch (start us, length us, event | category | flops | bytes accessed | tf_op | source)
XLA Modules:
  0.0 157.8 jit_solution(18156459698969855203)
XLA Ops:
  0.6 0.0 copy-start
  0.6 0.0 copy-start.1
  0.7 0.7 convert_element_type.34
  1.4 0.8 copy.21
  2.2 0.1 eq.42
  2.3 0.1 eq.38
  2.5 0.6 reduce-window.6
  3.1 0.2 slice_reduce_fusion.1
  3.3 0.1 fusion.2
  3.4 0.1 reduce_sum.30
  3.6 0.1 copy.23
  3.6 0.7 multiply_add_fusion
  4.3 0.1 select_reduce_fusion.1
  4.5 0.1 convert_element_type.36
  4.6 0.1 fusion
  4.6 0.8 broadcast_in_dim.34.g_ref
  5.4 0.0 copy-done
  5.4 1.6 %convolution_convert_fusion = bf16[384,1792]{1,0:T(8,128)(2,1)} fusion(pred[384,128]{1,0:T(8,128)(4,1)S(1)} %fusion, bf16[128,1792]{1,0:T(8,128)(2,1)S(1)} %copy-done), kind=kOutput, calls=%fused_computation | convolution fusion | flops 176848896 | bytes 1884160 | tf_op jit(solution)/shard_map/dot_general | solution.py:678
  7.0 0.0 copy-done.1
  7.0 1.6 %convolution_convert_fusion.1 = bf16[384,1792]{1,0:T(8,128)(2,1)} fusion(pred[384,128]{1,0:T(8,128)(4,1)S(1)} %fusion, bf16[128,1792]{1,0:T(8,128)(2,1)S(1)} %copy-done.1), kind=kOutput, calls=%fused_computation.1 | convolution fusion | flops 176848896 | bytes 1884160 | tf_op jit(solution)/shard_map/dot_general | solution.py:677
  8.6 145.7 %shard_map.86 = (bf16[8,48,1792]{2,1,0:T(8,128)(2,1)}, f32[8,48,128]{2,1,0:T(8,128)}) custom-call(bf16[8,48,1792]{2,1,0:T(8,128)(2,1)} %bitcast.21, bf16[8,48,1792]{2,1,0:T(8,128)(2,1)} %bitcast.20, bf16[8,48,128]{2,1,0:T(8,128)(2,1)} %broadcast_in_dim.34.g_ref, bf16[7168,256]{1,0:T(8,128)(2,1)} %bitcast.22, bf16[7168,256]{1,0:T(8,128)(2,1)} %bitcast.23, ...), custom_call_target="tpu_custom_call" | custom-call | tf_op jit(solution)/shard_map/pallas_call | solution.py:585
  154.3 0.0 copy-start.2
  154.3 2.6 %convolution_convert_fusion.2 = bf16[128,1792]{1,0:T(8,128)(2,1)} fusion(pred[384,128]{1,0:T(8,128)(4,1)S(1)} %fusion, bf16[384,1792]{1,0:T(8,128)(2,1)} %bitcast.25), kind=kOutput, calls=%fused_computation.2 | convolution fusion | flops 176390144 | bytes 1884160 | tf_op jit(solution)/shard_map/dot_general | solution.py:693
  156.9 0.0 copy-done.2
  156.9 0.1 slice_reduce_fusion
  157.0 0.1 broadcast_in_dim.35
  157.1 0.7 select_reduce_fusion
  (3 shorter events, 0.0 us)
Async XLA Ops:
  0.6 4.8 %copy-start = (bf16[128,1792]{1,0:T(8,128)(2,1)S(1)}, bf16[128,1792]{1,0:T(8,128)(2,1)}, u32[]{:S(2)}) copy-start(bf16[128,1792]{1,0:T(8,128)(2,1)} %param.8) | copy-start | bytes 1376260
  0.6 6.4 %copy-start.1 = (bf16[128,1792]{1,0:T(8,128)(2,1)S(1)}, bf16[128,1792]{1,0:T(8,128)(2,1)}, u32[]{:S(2)}) copy-start(bf16[128,1792]{1,0:T(8,128)(2,1)} %param.7) | copy-start | bytes 1376260
  154.3 2.6 %copy-start.2 = (f32[8,48,128]{2,1,0:T(8,128)S(1)}, f32[8,48,128]{2,1,0:T(8,128)}, u32[]{:S(2)}) copy-start(f32[8,48,128]{2,1,0:T(8,128)} %get-tuple-element.5) | copy-start | bytes 589828

commit v4 on v3

--- a/solution.py
+++ b/solution.py
@@ -310,18 +310,24 @@
     def block(which, group, owner):
         return pairs[which][1].at[group, :, cols(owner)]
 
-    def dispatch(which, source, target):
-        return remote(
-            pairs[which][0].at[target],
-            block(which, source, share),
+    def ahead(place):
+        return lax.rem(me + (place + n // 2 - 3) % (n - 1) + 1, n)
+
+    def behind(place):
+        return lax.rem(me + n - (place + n // 2 - 3) % (n - 1) - 1, n)
+
+    def dispatch(which, place):
+        return remote(
+            pairs[which][0].at[ahead(place)],
+            block(which, place, share),
             by_group,
-            which * n + source,
-            (target, share),
-        )
-
-    def gate_copy(source, target):
-        return remote(
-            g_ref.at[target], g_out.at[source], gates, source, (target, share)
+            which * n + place,
+            (ahead(place), share),
+        )
+
+    def gate_copy(place):
+        return remote(
+            g_ref.at[ahead(place)], g_out.at[place], gates, place, (ahead(place), share)
         )
 
     def along(which, group, sent, sems_of, peer):
@@ -357,12 +363,12 @@
     def across(group):
         return remote(far_put.at[group], far_got.at[group], across_sems, group, (me, far))
 
-    def home(source, target):
-        return remote(put.at[target], out.at[source], back, source, (target, share))
-
-    def grad_home(source, target):
-        return remote(
-            part_sum.at[target], grad_out.at[source], grads, source, (target, share)
+    def home(place, landing):
+        return remote(put.at[place], out.at[landing], back, place, (behind(place), share))
+
+    def grad_home(place, landing):
+        return remote(
+            part_sum.at[place], grad_out.at[landing], grads, place, (behind(place), share)
         )
 
     def nt(left, right):
@@ -370,30 +376,163 @@
             left, right, (((1,), (1,)), ((), ())), preferred_element_type=jnp.float32
         )
 
-    def project(step):
-        at = pl.ds(pl.multiple_of(step * depth, 128), depth)
-        piece = x_out[:, :, at].reshape(rows, depth)
-        pre[...] += jnp.dot(piece, gate_w[at, :], preferred_element_type=jnp.float32)
-        up[...] += jnp.dot(piece, up_w[at, :], preferred_element_type=jnp.float32)
+    few = n // 2
+
+    def lines(part_at):
+        return pl.ds(part_at * few * most, few * most)
+
+    def places(part_at):
+        return pl.ds(part_at * few, few)
+
+    def project(part_at, first, last):
+        @pl.loop(first, last)
+        def _(step):
+            at = pl.ds(pl.multiple_of(step * depth, 128), depth)
+            piece = x_out[places(part_at), :, at].reshape(few * most, depth)
+            to = lines(part_at)
+            pre[to, :] += jnp.dot(piece, gate_w[at, :], preferred_element_type=jnp.float32)
+            up[to, :] += jnp.dot(piece, up_w[at, :], preferred_element_type=jnp.float32)
+
+    def share_out(which, place):
+        along(which, place, share, to_far, far).start()
+        along(which, place, share, to_near, near).start()
+
+    def pass_on(which, place):
+        along(which, place, far, to_far, far).wait_recv()
+        along(which, place, far, passed, near).start()
+
+    def accept(which, place):
+        if place > 0:
+            dispatch(which, place).wait_recv()
+        share_out(which, place)
+        if place % few > 0:
+            pass_on(which, place - 1)
+
+    def settle(which, part_at):
+        pass_on(which, part_at * few + few - 1)
+
+        @pl.loop(part_at * few, part_at * few + few)
+        def _(place):
+            along(which, place, near, to_near, near).wait_recv()
+            along(which, place, 3 - share, passed, near).wait_recv()
+
+    def settle_gates(part_at):
+        @pl.loop(max(1, part_at * few), part_at * few + few)
+        def _(place):
+            gate_copy(place).wait_recv()
+
+    def down(part_at):
+        @pl.loop(0, 8)
+        def _(step):
+            at = pl.ds(pl.multiple_of(step * depth, 128), depth)
+            piece = dy_out[places(part_at), :, at].reshape(few * most, depth)
+            dz[lines(part_at), :] += nt(piece, down_w[:, at])
+
+    def part_near(part_at):
+        to = places(part_at)
+        return remote(part.at[to], part_got.at[0, to], parts, part_at, (me, near))
+
+    def part_far(part_at):
+        to = places(part_at)
+        return remote(part_sum.at[to], part_got.at[1, to], parts, 2 + part_at, (me, far))
+
+    def pointwise(part_at):
+        @pl.loop(part_at * few, part_at * few + few)
+        def _(place):
+            at = pl.ds(pl.multiple_of(place * most, 16), most)
+            pre_b, up_b, dz_b = pre[at, :], up[at, :], dz[at, :]
+            sigma = jax.nn.sigmoid(pre_b)
+            active = pre_b * sigma
+            row = jnp.sum(active * up_b * dz_b, axis=1, keepdims=True)
+            part[place] = jnp.broadcast_to(row, (most, 128))
+            scaled = g_out[place][:, :1].astype(jnp.float32) * dz_b
+            du[at, :] = (scaled * active).astype(du.dtype)
+            dp[at, :] = (scaled * up_b * sigma * (1.0 + pre_b * (1.0 - sigma))).astype(
+                dp.dtype
+            )
+
+        part_near(part_at).start()
+
+    def expand(part_at, wanted, store):
+        @pl.loop(0, 7)
+        def _(step):
+            at = pl.ds(pl.multiple_of(wanted * quarter + step * narrow, 128), narrow)
+            to = lines(part_at)
+            value = nt(dp[to, :], gate_w[at, :]) + nt(du[to, :], up_w[at, :])
+            store(
+                pl.ds(pl.multiple_of(step * narrow, 128), narrow),
+                value.reshape(few, most, narrow),
+            )
+
+    def for_near(part_at, slot):
+        def keep(at, value):
+            near_put[slot, places(part_at), :, at] = value.astype(near_put.dtype)
+
+        expand(part_at, 3 - share if slot == 0 else near, keep)
+
+        @pl.loop(part_at * few, part_at * few + few)
+        def _(place):
+            half(place, slot).start()
+
+    def for_self(part_at, slot):
+        def keep(at, value):
+            mine[slot, places(part_at), :, at] = value
+
+        expand(part_at, far if slot == 0 else share, keep)
+
+    def send_far(part_at):
+        to = places(part_at)
+        part_near(part_at).wait()
+        part_sum[to] = part[to] + part_got[0, to]
+        part_far(part_at).start()
+
+        @pl.loop(part_at * few, part_at * few + few)
+        def _(place):
+            half(place, 0).wait_recv()
+            far_put[place] = (
+                mine[0, place] + near_got[0, place].astype(jnp.float32)
+            ).astype(far_put.dtype)
+            across(place).start()
+
+    def send_grads(part_at):
+        to = places(part_at)
+        part_far(part_at).wait()
+        part_sum[to] = part_sum[to] + part_got[1, to]
+
+        @pl.loop(max(1, part_at * few), part_at * few + few)
+        def _(place):
+            grad_home(place, me).start()
+
+    def full_sum(place):
+        half(place, 1).wait_recv()
+        across(place).wait_recv()
+        pair = mine[1, place] + near_got[1, place].astype(jnp.float32)
+        put[place] = (pair + far_got[place].astype(jnp.float32)).astype(put.dtype)
+
+    def send_home(first, last):
+        @pl.loop(first, last)
+        def _(place):
+            full_sum(place)
+            home(place, me).start()
 
     greet(n, me, share, near, far)
     own_copies = [
-        pltpu.make_async_copy(src.at[me], block(which, me, share), own.at[which])
+        pltpu.make_async_copy(src.at[me], block(which, 0, share), own.at[which])
         for which, (src, _) in enumerate(pairs)
     ]
-    own_copies.append(pltpu.make_async_copy(g_ref.at[me], g_out.at[me], own.at[2]))
+    own_copies.append(pltpu.make_async_copy(g_ref.at[me], g_out.at[0], own.at[2]))
     for copy in own_copies:
         copy.start()
-    for which in range(2):
-
-        @pl.loop(1, n)
-        def _(step):
-            target = lax.rem(me + step, n)
-            dispatch(which, me, target).start()
-
-    @pl.loop(1, n)
-    def _(step):
-        gate_copy(me, lax.rem(me + step, n)).start()
+    for first, last in ((1, few), (few, n)):
+        for which in range(2):
+
+            @pl.loop(first, last)
+            def _(place):
+                dispatch(which, place).start()
+
+        @pl.loop(first, last)
+        def _(place):
+            gate_copy(place).start()
 
     for copy in loads:
         copy.start()
@@ -402,142 +541,53 @@
     dz[...] = jnp.zeros_like(dz)
     for copy in own_copies:
         copy.wait()
-
-    def share_out(which, group):
-        along(which, group, share, to_far, far).start()
-        along(which, group, share, to_near, near).start()
-
-    def pass_on(which, group):
-        along(which, group, far, to_far, far).wait_recv()
-        along(which, group, far, passed, near).start()
-
-    def settle(which):
-        @pl.loop(0, n)
-        def _(group):
-            along(which, group, near, to_near, near).wait_recv()
-            along(which, group, 3 - share, passed, near).wait_recv()
-
-    share_out(0, me)
-
-    @pl.loop(1, n)
-    def _(step):
-        group = lax.rem(me - step + n, n)
-        dispatch(0, group, me).wait_recv()
-        share_out(0, group)
-        pass_on(0, lax.rem(me - step + 1 + n, n))
-
-    share_out(1, me)
-    pass_on(0, lax.rem(me + 1, n))
-    settle(0)
+    for place in range(few):
+        accept(0, place)
+    accept(1, 0)
+    settle(0, 0)
     loads[0].wait()
     loads[1].wait()
-
-    @pl.loop(1, n)
-    def _(step):
-        project(step - 1)
-        group = lax.rem(me - step + n, n)
-        dispatch(1, group, me).wait_recv()
-        share_out(1, group)
-        pass_on(1, lax.rem(me - step + 1 + n, n))
-
-    @pl.loop(n - 1, 8)
-    def _(step):
-        project(step)
-
-    pass_on(1, lax.rem(me + 1, n))
-
-    @pl.loop(1, n)
-    def _(step):
-        gate_copy(lax.rem(me - step + n, n), me).wait_recv()
-
+    for place in range(1, few):
+        project(0, 8 * (place - 1) // (few - 1), 8 * place // (few - 1))
+        accept(1, place)
+    accept(0, few)
+    settle(1, 0)
+    settle_gates(0)
     loads[2].wait()
-    settle(1)
-
-    @pl.loop(0, 8)
-    def _(step):
-        at = pl.ds(pl.multiple_of(step * depth, 128), depth)
-        dz[...] += nt(dy_out[:, :, at].reshape(rows, depth), down_w[:, at])
-
-    @pl.loop(0, n)
-    def _(group):
-        at = pl.ds(pl.multiple_of(group * most, 16), most)
-        pre_b, up_b, dz_b = pre[at, :], up[at, :], dz[at, :]
-        sigma = jax.nn.sigmoid(pre_b)
-        active = pre_b * sigma
-        row = jnp.sum(active * up_b * dz_b, axis=1, keepdims=True)
-        part[group] = jnp.broadcast_to(row, (most, 128))
-        scaled = g_out[group][:, :1].astype(jnp.float32) * dz_b
-        du[at, :] = (scaled * active).astype(du.dtype)
-        dp[at, :] = (scaled * up_b * sigma * (1.0 + pre_b * (1.0 - sigma))).astype(dp.dtype)
-
-    part_near = remote(part, part_got.at[0], parts, 0, (me, near))
-    part_near.start()
-
-    def expand(which, store):
-        @pl.loop(0, 7)
-        def _(step):
-            at = pl.ds(pl.multiple_of(which * quarter + step * narrow, 128), narrow)
-            value = nt(dp[...], gate_w[at, :]) + nt(du[...], up_w[at, :])
-            store(
-                pl.ds(pl.multiple_of(step * narrow, 128), narrow),
-                value.reshape(n, most, narrow),
-            )
-
-    for slot, wanted in ((0, 3 - share), (1, near)):
-
-        def keep(at, value):
-            near_put[slot, :, :, at] = value.astype(near_put.dtype)
-
-        expand(wanted, keep)
-
-        @pl.loop(0, n)
-        def _(step):
-            half(lax.rem(me + 1 + step, n), slot).start()
-
-    for slot, wanted in ((0, far), (1, share)):
-
-        def keep_wide(at, value):
-            mine[slot, :, :, at] = value
-
-        expand(wanted, keep_wide)
-        if slot == 0:
-            part_near.wait()
-            part_sum[...] = part[...] + part_got[0]
-            part_far = remote(part_sum, part_got.at[1], parts, 1, (me, far))
-            part_far.start()
-
-            @pl.loop(0, n)
-            def _(step):
-                group = lax.rem(me + 1 + step, n)
-                half(group, 0).wait_recv()
-                far_put[group] = (
-                    mine[0, group] + near_got[0, group].astype(jnp.float32)
-                ).astype(far_put.dtype)
-                across(group).start()
-
-    part_far.wait()
-    part_sum[...] = part_sum[...] + part_got[1]
-
-    @pl.loop(1, n)
-    def _(step):
-        grad_home(me, lax.rem(me + step, n)).start()
-
-    def full_sum(group):
-        half(group, 1).wait_recv()
-        across(group).wait_recv()
-        pair = mine[1, group] + near_got[1, group].astype(jnp.float32)
-        put[group] = (pair + far_got[group].astype(jnp.float32)).astype(put.dtype)
-
-    @pl.loop(1, n)
-    def _(step):
-        group = lax.rem(me + step, n)
-        full_sum(group)
-        home(me, group).start()
-
-    full_sum(me)
+    down(0)
+    pointwise(0)
+    early = [
+        lambda: for_near(0, 0),
+        lambda: for_near(0, 1),
+        lambda: (for_self(0, 0), send_far(0)),
+    ]
+    for place in range(few + 1, n):
+        accept(0, place)
+        early[place - few - 1]()
+    accept(1, few)
+    settle(0, 1)
+    for_self(0, 1)
+    for place in range(few + 1, n):
+        project(1, 8 * (place - few - 1) // (few - 1), 8 * (place - few) // (few - 1))
+        accept(1, place)
+        if place == few + 1:
+            send_grads(0)
+        send_home(place - few, place - few + 1)
+    settle(1, 1)
+    settle_gates(1)
+    down(1)
+    pointwise(1)
+    for_near(1, 0)
+    for_near(1, 1)
+    for_self(1, 0)
+    send_far(1)
+    for_self(1, 1)
+    send_grads(1)
+    send_home(few, n)
+    full_sum(0)
     last_copies = [
-        pltpu.make_async_copy(put.at[me], out.at[me], own.at[0]),
-        pltpu.make_async_copy(part_sum.at[me], grad_out.at[me], own.at[1]),
+        pltpu.make_async_copy(put.at[0], out.at[me], own.at[0]),
+        pltpu.make_async_copy(part_sum.at[0], grad_out.at[me], own.at[1]),
     ]
     for copy in last_copies:
         copy.start()
@@ -546,29 +596,27 @@
     for which in range(2):
 
         @pl.loop(0, n)
-        def _(group):
-            along(which, group, share, to_far, far).wait_send()
-            along(which, group, share, to_near, near).wait_send()
-            along(which, group, far, passed, near).wait_send()
-            half(group, which).wait_send()
+        def _(place):
+            along(which, place, share, to_far, far).wait_send()
+            along(which, place, share, to_near, near).wait_send()
+            along(which, place, far, passed, near).wait_send()
+            half(place, which).wait_send()
 
         @pl.loop(1, n)
-        def _(step):
-            dispatch(which, me, lax.rem(me + step, n)).wait_send()
+        def _(place):
+            dispatch(which, place).wait_send()
 
     @pl.loop(0, n)
-    def _(group):
-        across(group).wait_send()
+    def _(place):
+        across(place).wait_send()
 
     @pl.loop(1, n)
-    def _(step):
-        target = lax.rem(me + step, n)
-        source = lax.rem(me - step + n, n)
-        gate_copy(me, target).wait_send()
-        home(me, target).wait_send()
-        grad_home(me, target).wait_send()
-        home(source, me).wait_recv()
-        grad_home(source, me).wait_recv()
+    def _(place):
+        gate_copy(place).wait_send()
+        home(place, me).wait_send()
+        grad_home(place, me).wait_send()
+        home(place, ahead(place)).wait_recv()
+        grad_home(place, ahead(place)).wait_recv()
 
 
 def fused(send_x, send_dy, send_g, gate_mat, up_mat, down_mat):
@@ -617,7 +665,7 @@
         + [dma((n,)), dma((n,)), dma((3,))]
         + [dma((2 * n,))] * 2
         + [dma((n,))] * 6
-        + [dma((2,))] * 2,
+        + [dma((4,))] * 2,
         compiler_params=pltpu.CompilerParams(
             collective_id=2, has_side_effects=True, vmem_limit_bytes=VMEM_BYTES
         ),
@@ -681,7 +729,7 @@
     send_x = send_x.reshape(n_experts, most_slots, quarter)
     send_dy = send_dy.reshape(n_experts, most_slots, quarter)
     weights = (w_gate[0], w_up[0], w_down[0])
-    if most_slots % 16 == 0 and n_experts <= 9 and quarter % 1792 == 0:
+    if most_slots % 16 == 0 and n_experts == 8 and quarter % 1792 == 0:
         wide_g = jnp.broadcast_to(
             send_g.astype(jnp.bfloat16).reshape(n_experts, most_slots, 1),
             (n_experts, most_slots, 128),

time: 158 us -> 165 us (1.044); the launches traced: 158 us -> 163 us
  Pallas kernels: 146 us -> 150 us
    pallas_call x1, Pallas kernels: 146 us -> 150 us  [fused(): pl.pallas_call(functools.partial(fused_kernel, n), out_shape=(jax.ShapeDt...]
where the time goes in v4:
time: 165 us; the launch traced here: 163 us
  Pallas kernels  150 us (91%)
  matrix products  5.81 us (4%)
  other arithmetic  3.07 us (2%)
  local copies, waits for them, and re-layouts  2.54 us (2%)
    pallas_call x1, Pallas kernels, fused(): pl.pallas_call(functools.partial(fused_kernel, n), out_shape=(jax.ShapeDt...  150 us

profile of v4, /device:TPU:13, one launch (start us, length us, event | category | flops | bytes accessed | tf_op | source)
XLA Modules:
  0.0 162.5 jit_solution(5116581546426386940)
XLA Ops:
  0.6 0.0 copy-start
  0.6 0.0 copy-start.1
  0.7 0.7 convert_element_type.34
  1.4 0.8 copy.21
  2.2 0.1 eq.42
  2.3 0.1 eq.38
  2.5 0.6 reduce-window.6
  3.1 0.2 slice_reduce_fusion.1
  3.3 0.1 fusion.2
  3.4 0.1 reduce_sum.30
  3.6 0.1 copy.23
  3.6 0.7 multiply_add_fusion
  4.3 0.1 select_reduce_fusion.1
  4.5 0.1 convert_element_type.36
  4.6 0.1 fusion
  4.6 0.8 broadcast_in_dim.34.g_ref
  5.4 0.0 copy-done
  5.4 1.6 convolution_convert_fusion
  7.0 0.0 copy-done.1
  7.0 1.6 convolution_convert_fusion.1
  8.6 150.4 %shard_map.86 = (bf16[8,48,1792]{2,1,0:T(8,128)(2,1)}, f32[8,48,128]{2,1,0:T(8,128)}) custom-call(bf16[8,48,1792]{2,1,0:T(8,128)(2,1)} %bitcast.21, bf16[8,48,1792]{2,1,0:T(8,128)(2,1)} %bitcast.20, bf16[8,48,128]{2,1,0:T(8,128)(2,1)} %broadcast_in_dim.34.g_ref, bf16[7168,256]{1,0:T(8,128)(2,1)} %bitcast.22, bf16[7168,256]{1,0:T(8,128)(2,1)} %bitcast.23, ...), custom_call_target="tpu_custom_call" | custom-call | tf_op jit(solution)/shard_map/pallas_call | solution.py:633
  159.0 0.0 copy-start.2
  159.0 2.6 %convolution_convert_fusion.2 = bf16[128,1792]{1,0:T(8,128)(2,1)} fusion(pred[384,128]{1,0:T(8,128)(4,1)S(1)} %fusion, bf16[384,1792]{1,0:T(8,128)(2,1)} %bitcast.25), kind=kOutput, calls=%fused_computation.2 | convolution fusion | flops 176390144 | bytes 1884160 | tf_op jit(solution)/shard_map/dot_general | solution.py:741
  161.6 0.0 copy-done.2
  161.6 0.1 slice_reduce_fusion
  161.7 0.1 broadcast_in_dim.35
  161.8 0.7 select_reduce_fusion
  (3 shorter events, 0.0 us)
Async XLA Ops:
  0.6 4.8 %copy-start = (bf16[128,1792]{1,0:T(8,128)(2,1)S(1)}, bf16[128,1792]{1,0:T(8,128)(2,1)}, u32[]{:S(2)}) copy-start(bf16[128,1792]{1,0:T(8,128)(2,1)} %param.8) | copy-start | bytes 1376260
  0.6 6.4 %copy-start.1 = (bf16[128,1792]{1,0:T(8,128)(2,1)S(1)}, bf16[128,1792]{1,0:T(8,128)(2,1)}, u32[]{:S(2)}) copy-start(bf16[128,1792]{1,0:T(8,128)(2,1)} %param.7) | copy-start | bytes 1376260
  159.0 2.6 %copy-start.2 = (f32[8,48,128]{2,1,0:T(8,128)S(1)}, f32[8,48,128]{2,1,0:T(8,128)}, u32[]{:S(2)}) copy-start(f32[8,48,128]{2,1,0:T(8,128)} %get-tuple-element.5) | copy-start | bytes 589828

commit v5 on v3

--- a/solution.py
+++ b/solution.py
@@ -310,6 +310,14 @@
     def block(which, group, owner):
         return pairs[which][1].at[group, :, cols(owner)]
 
+    shift = (share % 2) * (n // 2 - 1)
+
+    def ahead(step):
+        return lax.rem(me + (step - 1 + shift) % (n - 1) + 1, n)
+
+    def behind(step):
+        return lax.rem(me + n - (step - 1 + shift) % (n - 1) - 1, n)
+
     def dispatch(which, source, target):
         return remote(
             pairs[which][0].at[target],
@@ -388,8 +396,7 @@
 
         @pl.loop(1, n)
         def _(step):
-            target = lax.rem(me + step, n)
-            dispatch(which, me, target).start()
+            dispatch(which, me, ahead(step)).start()
 
     @pl.loop(1, n)
     def _(step):
@@ -421,13 +428,16 @@
 
     @pl.loop(1, n)
     def _(step):
-        group = lax.rem(me - step + n, n)
-        dispatch(0, group, me).wait_recv()
-        share_out(0, group)
-        pass_on(0, lax.rem(me - step + 1 + n, n))
+        dispatch(0, behind(step), me).wait_recv()
+        share_out(0, behind(step))
+
+        @pl.when(step > 1)
+        def _():
+            pass_on(0, behind(step - 1 + (n - 1)))
 
     share_out(1, me)
-    pass_on(0, lax.rem(me + 1, n))
+    pass_on(0, me)
+    pass_on(0, behind(n - 1))
     settle(0)
     loads[0].wait()
     loads[1].wait()
@@ -435,16 +445,19 @@
     @pl.loop(1, n)
     def _(step):
         project(step - 1)
-        group = lax.rem(me - step + n, n)
-        dispatch(1, group, me).wait_recv()
-        share_out(1, group)
-        pass_on(1, lax.rem(me - step + 1 + n, n))
+        dispatch(1, behind(step), me).wait_recv()
+        share_out(1, behind(step))
+
+        @pl.when(step > 1)
+        def _():
+            pass_on(1, behind(step - 1 + (n - 1)))
 
     @pl.loop(n - 1, 8)
     def _(step):
         project(step)
 
-    pass_on(1, lax.rem(me + 1, n))
+    pass_on(1, me)
+    pass_on(1, behind(n - 1))
 
     @pl.loop(1, n)
     def _(step):
@@ -506,15 +519,19 @@
             part_far = remote(part_sum, part_got.at[1], parts, 1, (me, far))
             part_far.start()
 
-            @pl.loop(0, n)
-            def _(step):
-                group = lax.rem(me + 1 + step, n)
+            def send_far(group):
                 half(group, 0).wait_recv()
                 far_put[group] = (
                     mine[0, group] + near_got[0, group].astype(jnp.float32)
                 ).astype(far_put.dtype)
                 across(group).start()
 
+            @pl.loop(1, n)
+            def _(step):
+                send_far(ahead(step))
+
+            send_far(me)
+
     part_far.wait()
     part_sum[...] = part_sum[...] + part_got[1]
 
@@ -530,9 +547,8 @@
 
     @pl.loop(1, n)
     def _(step):
-        group = lax.rem(me + step, n)
-        full_sum(group)
-        home(me, group).start()
+        full_sum(ahead(step))
+        home(me, ahead(step)).start()
 
     full_sum(me)
     last_copies = [

time: 158 us -> 158 us (level)
  no operation moved by 1% of the time
where the time goes in v5:
time: 158 us
  Pallas kernels  146 us (92%)
  matrix products  5.81 us (4%)
  other arithmetic  3.07 us (2%)
  local copies, waits for them, and re-layouts  2.54 us (2%)
    pallas_call x1, Pallas kernels, fused(): pl.pallas_call(functools.partial(fused_kernel, n), out_shape=(jax.ShapeDt...  146 us

profile of v5, /device:TPU:13, one launch (start us, length us, event | category | flops | bytes accessed | tf_op | source)
XLA Modules:
  0.0 157.7 jit_solution(7543629275422943050)
XLA Ops:
  0.6 0.0 copy-start
  0.6 0.0 copy-start.1
  0.7 0.7 convert_element_type.34
  1.4 0.8 copy.21
  2.2 0.1 eq.42
  2.3 0.1 eq.38
  2.5 0.6 reduce-window.6
  3.1 0.2 slice_reduce_fusion.1
  3.3 0.1 fusion.2
  3.4 0.1 reduce_sum.30
  3.6 0.1 copy.23
  3.6 0.7 multiply_add_fusion
  4.3 0.1 select_reduce_fusion.1
  4.5 0.1 convert_element_type.36
  4.6 0.1 fusion
  4.6 0.8 broadcast_in_dim.34.g_ref
  5.4 0.0 copy-done
  5.4 1.6 %convolution_convert_fusion = bf16[384,1792]{1,0:T(8,128)(2,1)} fusion(pred[384,128]{1,0:T(8,128)(4,1)S(1)} %fusion, bf16[128,1792]{1,0:T(8,128)(2,1)S(1)} %copy-done), kind=kOutput, calls=%fused_computation | convolution fusion | flops 176848896 | bytes 1884160 | tf_op jit(solution)/shard_map/dot_general | solution.py:694
  7.0 0.0 copy-done.1
  7.0 1.6 %convolution_convert_fusion.1 = bf16[384,1792]{1,0:T(8,128)(2,1)} fusion(pred[384,128]{1,0:T(8,128)(4,1)S(1)} %fusion, bf16[128,1792]{1,0:T(8,128)(2,1)S(1)} %copy-done.1), kind=kOutput, calls=%fused_computation.1 | convolution fusion | flops 176848896 | bytes 1884160 | tf_op jit(solution)/shard_map/dot_general | solution.py:693
  8.6 145.6 %shard_map.86 = (bf16[8,48,1792]{2,1,0:T(8,128)(2,1)}, f32[8,48,128]{2,1,0:T(8,128)}) custom-call(bf16[8,48,1792]{2,1,0:T(8,128)(2,1)} %bitcast.21, bf16[8,48,1792]{2,1,0:T(8,128)(2,1)} %bitcast.20, bf16[8,48,128]{2,1,0:T(8,128)(2,1)} %broadcast_in_dim.34.g_ref, bf16[7168,256]{1,0:T(8,128)(2,1)} %bitcast.22, bf16[7168,256]{1,0:T(8,128)(2,1)} %bitcast.23, ...), custom_call_target="tpu_custom_call" | custom-call | tf_op jit(solution)/shard_map/pallas_call | solution.py:601
  154.2 0.0 copy-start.2
  154.2 2.6 %convolution_convert_fusion.2 = bf16[128,1792]{1,0:T(8,128)(2,1)} fusion(pred[384,128]{1,0:T(8,128)(4,1)S(1)} %fusion, bf16[384,1792]{1,0:T(8,128)(2,1)} %bitcast.25), kind=kOutput, calls=%fused_computation.2 | convolution fusion | flops 176390144 | bytes 1884160 | tf_op jit(solution)/shard_map/dot_general | solution.py:709
  156.8 0.0 copy-done.2
  156.8 0.1 slice_reduce_fusion
  156.9 0.1 broadcast_in_dim.35
  157.0 0.7 select_reduce_fusion
  (3 shorter events, 0.0 us)
Async XLA Ops:
  0.6 4.8 %copy-start = (bf16[128,1792]{1,0:T(8,128)(2,1)S(1)}, bf16[128,1792]{1,0:T(8,128)(2,1)}, u32[]{:S(2)}) copy-start(bf16[128,1792]{1,0:T(8,128)(2,1)} %param.8) | copy-start | bytes 1376260
  0.6 6.4 %copy-start.1 = (bf16[128,1792]{1,0:T(8,128)(2,1)S(1)}, bf16[128,1792]{1,0:T(8,128)(2,1)}, u32[]{:S(2)}) copy-start(bf16[128,1792]{1,0:T(8,128)(2,1)} %param.7) | copy-start | bytes 1376260
  154.2 2.6 %copy-start.2 = (f32[8,48,128]{2,1,0:T(8,128)S(1)}, f32[8,48,128]{2,1,0:T(8,128)}, u32[]{:S(2)}) copy-start(f32[8,48,128]{2,1,0:T(8,128)} %get-tuple-element.5) | copy-start | bytes 589828

commit v6 on v3

--- a/solution.py
+++ b/solution.py
@@ -293,8 +293,8 @@
     )(contrib, partial_grad)
 
 
-def fused_kernel(n, x_ref, dy_ref, g_ref, gate_hbm, up_hbm, down_hbm, out, grad_out,
-                 x_out, dy_out, g_out, gate_w, up_w, down_w, pre, up, dz, dp, du,
+def fused_kernel(n, tok_ref, grad_ref, pick_ref, g_ref, gate_hbm, up_hbm, down_hbm, out, grad_out,
+                 x_ref, dy_ref, x_out, dy_out, g_out, gate_w, up_w, down_w, pre, up, dz, dp, du,
                  near_put, mine, near_got, far_put, far_got, put, part, part_got, part_sum,
                  load, *all_sems):
     sems, late = all_sems[:11], all_sems[11:]
@@ -377,19 +377,25 @@
         up[...] += jnp.dot(piece, up_w[at, :], preferred_element_type=jnp.float32)
 
     greet(n, me, share, near, far)
-    own_copies = [
-        pltpu.make_async_copy(src.at[me], block(which, me, share), own.at[which])
-        for which, (src, _) in enumerate(pairs)
-    ]
-    own_copies.append(pltpu.make_async_copy(g_ref.at[me], g_out.at[me], own.at[2]))
+    own_copies = [pltpu.make_async_copy(g_ref.at[me], g_out.at[me], own.at[2])]
     for copy in own_copies:
         copy.start()
+
+    def picked(which, target):
+        rows_of = (tok_ref, grad_ref)[which]
+        return jnp.dot(
+            pick_ref[target], rows_of[...], preferred_element_type=jnp.float32
+        ).astype(x_ref.dtype)
+
     for which in range(2):
 
         @pl.loop(1, n)
         def _(step):
             target = lax.rem(me + step, n)
+            pairs[which][0][target] = picked(which, target)
             dispatch(which, me, target).start()
+
+        pairs[which][1][me, :, cols(share)] = picked(which, me)
 
     @pl.loop(1, n)
     def _(step):
@@ -571,9 +577,10 @@
         grad_home(source, me).wait_recv()
 
 
-def fused(send_x, send_dy, send_g, gate_mat, up_mat, down_mat):
-    n, most, quarter = send_x.shape
-    kind = send_x.dtype
+def fused(tokens, out_grad, chooser, send_g, gate_mat, up_mat, down_mat):
+    n, most, _ = chooser.shape
+    quarter = tokens.shape[1]
+    kind = tokens.dtype
     hidden = gate_mat.shape[1]
     rows = n * most
     dma = pltpu.SemaphoreType.DMA
@@ -588,9 +595,11 @@
             jax.ShapeDtypeStruct((n, most, quarter), kind),
             jax.ShapeDtypeStruct(flat, jnp.float32),
         ),
-        in_specs=[VMEM] * 3 + [anywhere] * 3,
+        in_specs=[VMEM] * 4 + [anywhere] * 3,
         out_specs=[VMEM] * 2,
         scratch_shapes=[
+            stage,
+            stage,
             wide,
             wide,
             pltpu.VMEM(flat, kind),
@@ -621,7 +630,7 @@
         compiler_params=pltpu.CompilerParams(
             collective_id=2, has_side_effects=True, vmem_limit_bytes=VMEM_BYTES
         ),
-    )(send_x, send_dy, send_g, gate_mat, up_mat, down_mat)
+    )(tokens, out_grad, chooser, send_g, gate_mat, up_mat, down_mat)
 
 
 def in_steps(send_x, send_dy, send_g, gate_mat, up_mat, down_mat):
@@ -686,7 +695,13 @@
             send_g.astype(jnp.bfloat16).reshape(n_experts, most_slots, 1),
             (n_experts, most_slots, 128),
         )
-        returned, returned_grad = fused(send_x, send_dy, wide_g, *weights)
+        returned, returned_grad = fused(
+            tokens,
+            out_grad,
+            chooser.reshape(n_experts, most_slots, tok_rows),
+            wide_g,
+            *weights,
+        )
         returned_grad = returned_grad[:, :, 0]
     else:
         returned, returned_grad = in_steps(send_x, send_dy, send_g, *weights)

time: 158 us -> 156 us (0.987)
  matrix products: 5.81 us -> 2.6 us
    dot_general x2 -> x0, matrix products: 3.2 us -> none  [the longest x1 1.62 us: local(): jnp.dot(chooser, out_grad, preferred_element_type=jnp.float32)]
where the time goes in v6:
time: 156 us; the launch traced here: 155 us
  Pallas kernels  145 us (93%)
  other arithmetic  3.65 us (2%)
  matrix products  2.6 us (2%)
  local copies, waits for them, and re-layouts  2.51 us (2%)
    pallas_call x1, Pallas kernels, fused(): pl.pallas_call(functools.partial(fused_kernel, n), out_shape=(jax.ShapeDt...  145 us

profile of v6, /device:TPU:13, one launch (start us, length us, event | category | flops | bytes accessed | tf_op | source)
XLA Modules:
  0.0 154.9 jit_solution(3590155797388155691)
XLA Ops:
  0.6 0.7 convert_element_type.34
  1.3 0.8 copy.21
  2.1 0.1 eq.42
  2.2 0.1 eq.38
  2.4 0.6 reduce-window.6
  3.0 0.2 slice_reduce_fusion.1
  3.2 0.1 fusion.2
  3.3 0.1 reduce_sum.30
  3.5 0.1 copy.23
  3.5 0.7 multiply_add_fusion
  4.2 0.1 select_reduce_fusion.1
  4.4 0.1 convert_element_type.36
  4.5 0.1 fusion
  4.5 0.7 broadcast_in_dim.34.g_ref
  5.3 0.7 convert_element_type.38
  5.9 145.4 %shard_map.86 = (bf16[8,48,1792]{2,1,0:T(8,128)(2,1)}, f32[8,48,128]{2,1,0:T(8,128)}) custom-call(bf16[128,1792]{1,0:T(8,128)(2,1)} %tok_ref.1, bf16[128,1792]{1,0:T(8,128)(2,1)} %grad_ref.1, bf16[8,48,128]{2,1,0:T(8,128)(2,1)} %bitcast.19, bf16[8,48,128]{2,1,0:T(8,128)(2,1)} %broadcast_in_dim.34.g_ref, bf16[7168,256]{1,0:T(8,128)(2,1)} %bitcast.15, ...), custom_call_target="tpu_custom_call" | custom-call | tf_op jit(solution)/shard_map/pallas_call | solution.py:592
  151.4 0.0 copy-start
  151.4 2.6 %convolution_convert_fusion = bf16[128,1792]{1,0:T(8,128)(2,1)} fusion(pred[384,128]{1,0:T(8,128)(4,1)S(1)} %fusion, bf16[384,1792]{1,0:T(8,128)(2,1)} %bitcast.18), kind=kOutput, calls=%fused_computation | convolution fusion | flops 176390144 | bytes 1884160 | tf_op jit(solution)/shard_map/dot_general | solution.py:708
  154.0 0.0 copy-done
  154.0 0.1 slice_reduce_fusion
  154.1 0.1 broadcast_in_dim.35
  154.2 0.7 select_reduce_fusion
  (3 shorter events, 0.0 us)
Async XLA Ops:
  151.4 2.6 %copy-start = (f32[8,48,128]{2,1,0:T(8,128)S(1)}, f32[8,48,128]{2,1,0:T(8,128)}, u32[]{:S(2)}) copy-start(f32[8,48,128]{2,1,0:T(8,128)} %get-tuple-element.5) | copy-start | bytes 589828
